TPU v7x, 768 devices: a whole 4x8x12 slice. The times are simulated.
768 devices in a mesh: slab: 64 (over y, x, core), sub: 12 (over z).
Axes of the slice: x: 4, y: 8, z: 12, core: 2. Of those that a mesh axis runs over, the one named last changes fastest.
Arguments:
- field_init: float32 [3, 512, 192, 128], P(None, 'slab', 'sub'), may hold values from -6 to 6
- load: float32 [3, 512, 192, 128], P(None, 'slab', 'sub'), may hold values from -6 to 6
- modulus: float32 [512, 192, 128], P('slab', 'sub'), may hold values from 0.3 to 3
- seg_z: int32 [512], P('slab'), may hold values from 0 to 127, as said below
- seg_y: int32 [192], P('sub'), may hold values from 0 to 47, as said below
- seg_x: int32 [128], replicated, may hold values from 0 to 31, as said below
Outputs:
- smoothed: float32 [3, 512, 192, 128], P(None, 'slab', 'sub')
- coarse: float32 [6, 128, 1536], P(None, 'slab', 'sub')
Inputs may be any that keep to these rules, and one draw needn't show every extreme that they name: `seg_z`: along z, segment k starts at node 4 k or 4 k + 1 (segment 0 at 0, the last segment at 4 k + 1) and runs to the next start or the grid's end; entries never fall. `seg_y`: along y, segment k starts at node 4 k or 4 k + 1 (segment 0 at 0, the last segment at 4 k + 1) and runs to the next start or the grid's end; entries never fall. `seg_x`: along x, segment k starts at node 4 k or 4 k + 1 (segment 0 at 0, the last segment at 4 k + 1) and runs to the next start or the grid's end; entries never fall.
All inputs are finite; a program needn't handle non-finite values.
Results may differ from a plain program's by a relative error of at most 0.0003.
Values sent between devices are 32-bit elements; how exact they have to be, the bound alone decides.
No kernel may reach another device: no remote copies, remote signals or barrier semaphores. Data moves between devices by JAX's collectives and lax.ppermute only.
A program may use at most 32 MiB of HBM per device.

v0:
```python
import jax
import jax.numpy as jnp
from jax import lax
from jax.experimental import pallas as pl
from jax.experimental.pallas import tpu as pltpu
from jax.sharding import PartitionSpec as P


SX = 32
SY = 4
SZ = 2
DEPTH = 8
ROWS = 16
WIDTH = 128
TALL = 24
DAMPING = 0.6

POISSON = 0.3
LAME = POISSON / ((1.0 + POISSON) * (1.0 - 2.0 * POISSON))
SHEAR = 0.5 / (1.0 + POISSON)

FIELD, LOAD, MODULUS = 0, 24, 48
PAIRS = 28
UP_PLANES = (
    [(FIELD, c, z) for c in range(3) for z in (5, 6, 7)]
    + [(LOAD, c, z) for c in range(3) for z in (6, 7)]
    + [(MODULUS, 0, z) for z in (5, 6, 7)]
)
DOWN_PLANES = (
    [(FIELD, c, z) for c in range(3) for z in (0, 1, 2, 3)]
    + [(LOAD, c, z) for c in range(3) for z in (0, 1, 2)]
    + [(MODULUS, 0, z) for z in (0, 1, 2)]
)


def y_slot(kind, c, z):
    index = kind + DEPTH * c + z
    return index // 2, 4 * (index % 2)


def is_even(axis):
    return lax.axis_index(axis) % 2 == 0


def pack_y(
    seg_y_hbm, seg_z_hbm, seg_x_hbm, field_hbm, load_hbm, modulus_hbm,
    first, second, field, load, modulus, labels, seg_y, seg_z, seg_x, sems,
):
    pairs = (
        (field_hbm, field), (load_hbm, load), (modulus_hbm, modulus),
        (seg_y_hbm, seg_y), (seg_z_hbm, seg_z), (seg_x_hbm, seg_x),
    )
    copies = [pltpu.make_async_copy(src, dst, sems.at[k]) for k, (src, dst) in enumerate(pairs)]
    for copy in copies:
        copy.start()
    even = is_even("sub")
    parts = ((field, FIELD, 3), (load, LOAD, 3), (modulus, MODULUS, 1))
    for copy, (ref, kind, comps) in zip(copies, parts):
        copy.wait()
        for c in range(comps):
            for z in range(DEPTH):
                tile, row = y_slot(kind, c, z)
                plane = ref[c, z] if comps == 3 else ref[z]
                up, down = plane[12:16], plane[0:4]
                first[tile, row : row + 4, :] = jnp.where(even, up, down)
                second[tile, row : row + 4, :] = jnp.where(even, down, up)
    for copy in copies[3:]:
        copy.wait()
    label = jnp.full((8, WIDTH), seg_y[0].astype(jnp.float32))
    first[PAIRS] = label
    second[PAIRS] = label
    for k in range(SY):
        labels[k : k + 1, :] = jnp.full((1, WIDTH), seg_y[4 * k].astype(jnp.float32))
    for k in range(SZ):
        labels[SY + k : SY + k + 1, :] = jnp.full((1, WIDTH), seg_z[4 * k].astype(jnp.float32))
    labels[7:8, :] = seg_x[...].reshape(1, WIDTH).astype(jnp.float32)


def edge_tile(even, first, second, kind, c, z):
    tile, row = y_slot(kind, c, z)
    one, two = first[tile, row : row + 4, :], second[tile, row : row + 4, :]
    above, below = jnp.where(even, one, two), jnp.where(even, two, one)
    return jnp.concatenate([above, below], axis=0)


def pack_z(labels, field, load, modulus, y_first, y_second, first, second):
    even_y, even_z = is_even("sub"), is_even("slab")
    tall = {}

    def whole(kind, c, z):
        if (kind, c, z) not in tall:
            own = (field if kind == FIELD else load)[c, z] if kind != MODULUS else modulus[z]
            tall[kind, c, z] = jnp.concatenate(
                [own, edge_tile(even_y, y_first, y_second, kind, c, z)], axis=0
            )
        return tall[kind, c, z]

    for index, plane in enumerate(DOWN_PLANES):
        down = whole(*plane)
        if index < len(UP_PLANES):
            up = whole(*UP_PLANES[index])
            first[index] = jnp.where(even_z, up, down)
            second[index] = jnp.where(even_z, down, up)
        else:
            first[index] = down
            second[index] = down
    label = jnp.broadcast_to(labels[SY : SY + 1, :], (TALL, WIDTH))
    first[len(DOWN_PLANES)] = label
    second[len(DOWN_PLANES)] = label


def roll_x(value, shift):
    return pltpu.roll(value, shift % WIDTH, 1)


def roll_y(value, shift):
    return pltpu.roll(value, shift % TALL, 0)


class Planes:
    def __init__(self, mine, offset, given=None):
        self.mine, self.offset, self.given = mine, offset, given
        self.written = set()

    def where(self, lead, z, tile, ref, offset):
        rows = slice(None) if tile is None else slice(8 * tile, 8 * tile + 8)
        return ref, (*lead, z + offset, rows, slice(None))

    def load(self, *lead, z, tile=None):
        own = {(*lead, z, t) in self.written for t in (range(3) if tile is None else (tile,))}
        assert len(own) == 1
        if own.pop():
            ref, at = self.where(lead, z, tile, self.mine, self.offset)
        else:
            ref, at = self.where(lead, z, tile, self.given, 0)
        return ref[at]

    def store(self, value, *lead, z, tile=None):
        self.written |= {(*lead, z, t) for t in (range(3) if tile is None else (tile,))}
        ref, at = self.where(lead, z, tile, self.mine, self.offset)
        ref[at] = value


def fill(state, planes, own_block=None, z_part=None):
    work, loads, elem = state[:3]
    slab_pos, sub_pos = lax.axis_index("slab"), lax.axis_index("sub")
    last_slab, last_sub = lax.axis_size("slab") - 1, lax.axis_size("sub") - 1

    def gather(kind, c, z):
        if z < 0:
            return z_part[UP_PLANES.index((kind, c, z + DEPTH))]
        if z >= DEPTH:
            return z_part[DOWN_PLANES.index((kind, c, z - DEPTH))]
        field, load, modulus, y_first, y_second = own_block
        own = (field if kind == FIELD else load)[c, z] if kind != MODULUS else modulus[z]
        return jnp.concatenate([own, edge_tile(is_even("sub"), y_first, y_second, kind, c, z)], axis=0)

    row = lax.broadcasted_iota(jnp.int32, (TALL, WIDTH), 0)
    lane = lax.broadcasted_iota(jnp.int32, (TALL, WIDTH), 1)
    inside = (lane < WIDTH - 1) & ((row != ROWS - 1) | (sub_pos != last_sub))
    inside_top = inside & (slab_pos != last_slab)
    for z in planes:
        if -3 <= z <= 10:
            value = gather(MODULUS, 0, z)
            elem.store(jnp.where(inside_top if z == DEPTH - 1 else inside, value, 0.0), z=z)
        for c in range(3):
            work.store(gather(FIELD, c, z), c, z=z)
            if -2 <= z <= 10:
                loads.store(gather(LOAD, c, z), c, z=z)


def invert(state, first, last):
    elem, inv = state[2], state[3]
    diag_scale = (LAME + 4.0 * SHEAR) / 9.0
    off_scale = (LAME + SHEAR) / 12.0
    before = None
    for z in range(first - 1, last + 1):
        e = elem.load(z=z)
        right = roll_x(e, 1)
        sum_x, dif_x = e + right, right - e
        sum_up, dif_up = roll_y(sum_x, 1), roll_y(dif_x, 1)
        now = (sum_up + sum_x, sum_up - sum_x, dif_up + dif_x, dif_up - dif_x)
        if before is not None:
            p = diag_scale * (before[0] + now[0])
            cc = off_scale * (before[1] - now[1])
            b = off_scale * (before[2] - now[2])
            a = off_scale * (before[3] + now[3])
            pp = p * p
            co00, co11, co22 = pp - cc * cc, pp - b * b, pp - a * a
            co01, co02, co12 = b * cc - a * p, a * cc - b * p, a * b - p * cc
            det = p * co00 + a * co01 + b * co02
            scale = jnp.where(det != 0.0, DAMPING / det, 0.0)
            for k, value in enumerate((co00, co01, co02, co11, co12, co22)):
                inv.store(value * scale, k, z=z)
        before = now


def spread(state, planes):
    work, modes = state[0], state[4]
    for c in range(3):
        for z in planes:
            v = work.load(c, z=z)
            left = roll_x(v, -1)
            sum_x, dif_x = v + left, left - v
            sum_up, dif_up = roll_y(sum_x, -1), roll_y(dif_x, -1)
            modes.store(sum_x + sum_up, 4 * c, z=z)
            modes.store(dif_x + dif_up, 4 * c + 1, z=z)
            modes.store(sum_up - sum_x, 4 * c + 2, z=z)
            modes.store(dif_up - dif_x, 4 * c + 3, z=z)


def stress(state, lo, hi, resume=False, join=False):
    elem, modes, forces = state[2], state[4], state[5]
    for tile in range(3):
        old = [modes.load(k, z=lo, tile=tile) for k in range(12)]
        held = [forces.load(k, z=lo, tile=tile) for k in range(12)] if resume else None
        for z in range(lo, hi):
            e = elem.load(z=z, tile=tile)
            new = [modes.load(k, z=z + 1, tile=tile) for k in range(12)]
            total = [None if k % 4 == 0 else new[k] + old[k] for k in range(12)]
            delta = [new[k] - old[k] for k in range(12)]
            xa, xb, xc = total[1], total[2], total[3]
            xd, xe, xf, xg = delta[0], delta[1], delta[2], delta[3]
            ya, yb, yc = total[5], total[6], total[7]
            yd, ye, yf, yg = delta[4], delta[5], delta[6], delta[7]
            za, zb, zc = total[9], total[10], total[11]
            zd, ze, zf, zg = delta[8], delta[9], delta[10], delta[11]
            lam0, mu0 = e * (LAME / 16.0), e * (SHEAR / 16.0)
            lam1, mu1 = e * (LAME / 48.0), e * (SHEAR / 48.0)
            twice = e * (SHEAR / 8.0)
            last_scale = e * ((LAME + 4.0 * SHEAR) / 144.0)
            t = lam0 * (xa + yb + zd)
            xy, xz, yz = mu0 * (xb + ya), mu0 * (xd + za), mu0 * (yd + zb)
            s_x, s_y, s_z = lam1 * (yc + ze), lam1 * (xc + zf), lam1 * (xe + yf)
            q = xf + ye + zc
            even = (
                None, t + twice * xa, xy, s_y + mu0 * xc,
                None, xy, t + twice * yb, s_x + mu0 * yc,
                None, xz, yz, mu1 * (q + zc),
            )
            odd = (
                xz, s_z + mu0 * xe, mu1 * (q + xf), last_scale * xg,
                yz, mu1 * (q + ye), s_z + mu0 * yf, last_scale * yg,
                t + twice * zd, s_x + mu0 * ze, s_y + mu0 * zf, last_scale * zg,
            )
            for k in range(12):
                low = -odd[k] if even[k] is None else even[k] - odd[k]
                forces.store(low if held is None else held[k] + low, k, z=z, tile=tile)
            held = [odd[k] if even[k] is None else even[k] + odd[k] for k in range(12)]
            old = new
        for k in range(12):
            total = forces.load(k, z=hi, tile=tile) + held[k] if join else held[k]
            forces.store(total, k, z=hi, tile=tile)


def misfit(state, z):
    loads, forces = state[1], state[5]
    out = []
    for c in range(3):
        f = [forces.load(4 * c + k, z=z) for k in range(4)]
        sum_x = (f[0] - f[2]) + roll_y(f[0] + f[2], 1)
        dif_x = (f[1] - f[3]) + roll_y(f[1] + f[3], 1)
        out.append(loads.load(c, z=z) - ((sum_x - dif_x) + roll_x(sum_x + dif_x, 1)))
    return out


def relax(state, planes):
    work, inv = state[0], state[3]
    table = ((0, 1, 2), (1, 3, 4), (2, 4, 5))
    for z in planes:
        m = [inv.load(k, z=z) for k in range(6)]
        r = misfit(state, z)
        for c in range(3):
            i, j, k = table[c]
            step = m[i] * r[0] + m[j] * r[1] + m[k] * r[2]
            work.store(work.load(c, z=z) + step, c, z=z)


def solve_inner(field, load, modulus, y_first, y_second, *refs):
    state = [Planes(ref, 0) for ref in refs[:6]]
    residual = refs[6]
    fill(state, range(0, 8), own_block=(field, load, modulus, y_first, y_second))
    invert(state, 1, 7)
    spread(state, range(0, 8))
    stress(state, 0, 7)
    relax(state, range(1, 7))
    spread(state, range(1, 7))
    stress(state, 1, 6)
    relax(state, range(2, 6))
    spread(state, range(2, 6))
    stress(state, 2, 5)
    for z in (3, 4):
        for c, value in enumerate(misfit(state, z)):
            residual[c, z - 3] = value


LOWER, UPPER = (0, 1), (6, 7)
LOWER_REST, UPPER_REST = (0, 1, 2), (5, 6, 7, 8)


def solve_side(lower, z_part, given, mine, smooth, residual, smooth_from, residual_from):
    state = [Planes(ref, 3, old) for ref, old in zip(mine, given)]
    if lower:
        fill(state, range(-3, 0), z_part=z_part)
        invert(state, -2, 0)
        for first, last in ((-3, 0), (-2, 1), (-1, 2)):
            spread(state, range(first, last))
            stress(state, first, last, join=True)
            if last < 2:
                relax(state, range(first + 1, last + 1))
    else:
        fill(state, range(8, 12), z_part=z_part)
        invert(state, 8, 10)
        for first, last in ((7, 11), (6, 10), (5, 9)):
            spread(state, range(first + 1, last + 1))
            stress(state, first, last, resume=True)
            if last > 9:
                relax(state, range(first, last))
    for k, z in enumerate(LOWER if lower else UPPER):
        for c in range(3):
            smooth[c, smooth_from + k] = state[0].load(c, z=z)[:ROWS]
    for k, z in enumerate(LOWER_REST if lower else UPPER_REST):
        for c, value in enumerate(misfit(state, z)):
            residual[c, residual_from + k] = value


def solve_near(z_first, *refs):
    given, (smooth, residual), mine = refs[:6], refs[6:8], refs[8:14]
    for lower in (False, True):

        @pl.when(is_even("slab") != lower)
        def side():
            solve_side(lower, z_first, given, mine, smooth, residual, 0, 0)


def solve_far(labels, y_first, y_second, z_first, z_second, *refs):
    given, (middle, near_smooth, near_residual) = refs[:6], refs[6:9]
    (smooth, coarse), rows, residual, mine = refs[9:11], refs[11], refs[12], refs[13:19]
    slab_pos, sub_pos = lax.axis_index("slab"), lax.axis_index("sub")
    last_slab, last_sub = lax.axis_size("slab") - 1, lax.axis_size("sub") - 1
    even_y, even_z = is_even("sub"), is_even("slab")
    row = lax.broadcasted_iota(jnp.int32, (TALL, WIDTH), 0)
    for lower in (True, False):

        @pl.when(even_z == lower)
        def side():
            far, far_rest = (LOWER, LOWER_REST) if lower else (UPPER, UPPER_REST)
            near, near_rest = (UPPER, UPPER_REST) if lower else (LOWER, LOWER_REST)
            solve_side(lower, z_second, given, mine, smooth, residual, far[0], far_rest[0])
            for c in range(3):
                for k, z in enumerate(near):
                    smooth[c, z] = near_smooth[c, k]
                for k, z in enumerate(near_rest):
                    residual[c, z] = near_residual[c, k]

    for c in range(3):
        for z in range(2, 6):
            smooth[c, z] = given[0][c, z, :ROWS, :]
        for k in range(2):
            residual[c, 3 + k] = middle[c, k]

    def flag(value, segment):
        return jnp.where(value == segment.astype(jnp.float32), 1.0, 0.0)

    start_z = SZ * slab_pos
    owns_low = flag(labels[SY : SY + 1, :], start_z)
    mid_low = flag(labels[SY + 1 : SY + 2, :], start_z)
    mid_high = flag(labels[SY + 1 : SY + 2, :], start_z + 1)
    label = len(DOWN_PLANES)
    next_seg = jnp.where(even_z, z_first[label], z_second[label])[0:1]
    is_last_slab = slab_pos == last_slab
    owns_high = jnp.where(
        (next_seg == (start_z + 1).astype(jnp.float32)) & jnp.logical_not(is_last_slab), 1.0, 0.0
    )
    plane_weight = {
        (0, 0): owns_low, (0, 1): None, (0, 2): None, (0, 3): None, (0, 4): mid_low,
        (1, 4): mid_high, (1, 5): None, (1, 6): None, (1, 7): None, (1, 8): owns_high,
    }
    sums = [[None] * 5 for _ in range(SZ)]

    def restrict(z, r):
        for kz in range(SZ):
            if (kz, z) not in plane_weight:
                continue
            weight = plane_weight[kz, z]
            mine = r if weight is None else [weight * value for value in r]
            q = 0.5 * (z - 4 * kz - 2)
            terms = [mine[0], mine[1], mine[2], q * mine[1], q * mine[0]]
            for k in range(5):
                if k > 2 and q == 0.0:
                    continue
                sums[kz][k] = terms[k] if sums[kz][k] is None else sums[kz][k] + terms[k]

    for z in range(DEPTH + 1):
        restrict(z, [residual[c, z] for c in range(3)])
    count_z = [owns_low + 3.0 + mid_low, mid_high + 3.0 + owns_high]
    moment_z = [mid_low - owns_low, owns_high - mid_high]

    start_y = SY * sub_pos
    next_row = jnp.where(even_y, y_first[PAIRS], y_second[PAIRS])[0:1]
    owns_next = jnp.where(
        (next_row == (start_y + SY - 1).astype(jnp.float32)) & (sub_pos != last_sub), 1.0, 0.0
    )
    group = lax.broadcasted_iota(jnp.int32, (1, WIDTH), 1) // SX
    x = lax.broadcasted_iota(jnp.int32, (1, WIDTH), 1)
    seg_x = labels[7:8, :]
    q_x = 0.5 * (x.astype(jnp.float32) - 4.0 * seg_x - 2.0)
    count_y = jnp.zeros((1, WIDTH), jnp.float32)
    moment_y = jnp.zeros((1, WIDTH), jnp.float32)
    rows[...] = jnp.zeros((16 * SY, WIDTH), jnp.float32)
    for ky in range(SY):
        first = flag(labels[ky : ky + 1, :], start_y + ky)
        if ky < SY - 1:
            final = flag(labels[ky + 1 : ky + 2, :], start_y + ky)
        else:
            final = owns_next
        local = row - 4 * ky
        weight = jnp.where((local > 0) & (local < 4), 1.0, 0.0)
        weight = jnp.where(local == 0, first, jnp.where(local == 4, final, weight))
        moment = weight * (0.5 * (local - 2).astype(jnp.float32))
        count_y = jnp.where(group == ky, first + 3.0 + final, count_y)
        moment_y = jnp.where(group == ky, final - first, moment_y)
        total = lambda value: jnp.sum(value, axis=0, keepdims=True)
        for kz in range(SZ):
            r0, r1, r2, z1, z0 = sums[kz]
            plain = [total(weight * value) for value in (r0, r1, r2)]
            turned = [
                total(moment * r2 - weight * z1),
                total(weight * z0) - q_x * plain[2],
                q_x * plain[1] - total(moment * r0),
            ]
            for k, value in enumerate(plain + turned):
                rows[16 * ky + 6 * kz + k : 16 * ky + 6 * kz + k + 1, :] = value
        rows[16 * ky + 12 : 16 * ky + 13, :] = jnp.ones((1, WIDTH), jnp.float32)
        rows[16 * ky + 13 : 16 * ky + 14, :] = q_x

    target = lax.broadcasted_iota(jnp.int32, (WIDTH, WIDTH), 0) % SX
    chosen = jnp.where(target.astype(jnp.float32) == seg_x, 1.0, 0.0)
    totals = lax.dot_general(
        rows[...], chosen, (((1,), (1,)), ((), ())),
        precision=lax.Precision.HIGHEST, preferred_element_type=jnp.float32,
    )
    final_sums = totals[0:16]
    for ky in range(1, SY):
        final_sums = jnp.where(group == ky, totals[16 * ky : 16 * ky + 16], final_sums)
    count_x, moment_x = final_sums[12:13], final_sums[13:14]
    for kz in range(SZ):
        count = count_x * count_y * count_z[kz]
        centre = [
            moment_x * count_y * count_z[kz] / count,
            count_x * moment_y * count_z[kz] / count,
            count_x * count_y * moment_z[kz] / count,
        ]
        scale = 1.0 / jnp.sqrt(count)
        s = [final_sums[6 * kz + k : 6 * kz + k + 1] for k in range(6)]
        turned = [
            s[3] - (centre[1] * s[2] - centre[2] * s[1]),
            s[4] - (centre[2] * s[0] - centre[0] * s[2]),
            s[5] - (centre[0] * s[1] - centre[1] * s[0]),
        ]
        for k, value in enumerate(s[:3] + turned):
            coarse[k, kz : kz + 1, :] = value * scale


VMEM = pl.BlockSpec(memory_space=pltpu.VMEM)


def f32(*shape):
    return jax.ShapeDtypeStruct(shape, jnp.float32)


def scratch(*shape):
    return pltpu.VMEM(shape, jnp.float32)


def on_device(field_init, load, modulus, seg_z, seg_y, seg_x):
    def exchange(first, second, axis):
        count = lax.axis_size(axis)
        outcome = []
        for block, start in ((second, 1), (first, 0)):
            pairs = [(i, i + 1) for i in range(start, count - 1, 2)]
            outcome.append(lax.ppermute(block, axis, pairs + [(j, i) for i, j in pairs]))
        return outcome[1], outcome[0]

    def limit(mib):
        return pltpu.CompilerParams(vmem_limit_bytes=mib << 20)

    hbm = pl.BlockSpec(memory_space=pltpu.MemorySpace.HBM)
    blocks = [f32(3, DEPTH, ROWS, WIDTH), f32(3, DEPTH, ROWS, WIDTH), f32(DEPTH, ROWS, WIDTH)]
    arguments = (seg_y, seg_z, seg_x, field_init, load, modulus)
    *packed, field_init, load, modulus, labels = pl.pallas_call(
        pack_y,
        out_shape=[f32(PAIRS + 1, 8, WIDTH)] * 2 + blocks + [f32(8, WIDTH)],
        in_specs=[hbm] * 6,
        out_specs=[VMEM] * 6,
        scratch_shapes=[
            pltpu.SMEM((ROWS,), jnp.int32),
            pltpu.SMEM((DEPTH,), jnp.int32),
            pltpu.VMEM((WIDTH,), jnp.int32),
            pltpu.SemaphoreType.DMA((6,)),
        ],
        compiler_params=limit(4),
        name="pack_y",
    )(*[pltpu.with_memory_space_constraint(value, pltpu.MemorySpace.HBM) for value in arguments])
    y_parts = exchange(*packed, "sub")
    packed = pl.pallas_call(
        pack_z,
        out_shape=(f32(len(DOWN_PLANES) + 1, TALL, WIDTH),) * 2,
        in_specs=[VMEM] * 6,
        out_specs=(VMEM, VMEM),
        compiler_params=limit(4),
        name="pack_z",
    )(labels, field_init, load, modulus, *y_parts)
    z_parts = exchange(*packed, "slab")

    def sizes(planes):
        return [(3, planes, TALL, WIDTH)] * 2 + [(planes, TALL, WIDTH)] + [
            (n, planes, TALL, WIDTH) for n in (6, 12, 12)
        ]

    *state, middle = pl.pallas_call(
        solve_inner,
        out_shape=[f32(*size) for size in sizes(DEPTH)] + [f32(3, 2, TALL, WIDTH)],
        in_specs=[VMEM] * 5,
        out_specs=[VMEM] * 7,
        compiler_params=limit(6),
        name="solve_inner",
    )(field_init, load, modulus, *y_parts)
    near = pl.pallas_call(
        solve_near,
        out_shape=(f32(3, 2, ROWS, WIDTH), f32(3, 4, TALL, WIDTH)),
        in_specs=[VMEM] * 7,
        out_specs=(VMEM, VMEM),
        scratch_shapes=[scratch(*size) for size in sizes(15)],
        compiler_params=limit(12),
        name="solve_near",
    )(z_parts[0], *state)
    return pl.pallas_call(
        solve_far,
        out_shape=(f32(3, DEPTH, ROWS, WIDTH), f32(6, SZ, SY * SX)),
        in_specs=[VMEM] * 14,
        out_specs=(VMEM, VMEM),
        scratch_shapes=[scratch(16 * SY, WIDTH), scratch(3, 9, TALL, WIDTH)]
        + [scratch(*size) for size in sizes(15)],
        compiler_params=limit(14),
        name="solve_far",
    )(labels, *y_parts, *z_parts, *state, middle, *near)


def solution(mesh):
    in_specs = (
        P(None, "slab", "sub", None),
        P(None, "slab", "sub", None),
        P("slab", "sub", None),
        P("slab"),
        P("sub"),
        P(),
    )
    out_specs = (P(None, "slab", "sub", None), P(None, "slab", "sub"))
    return jax.shard_map(
        on_device, mesh=mesh, in_specs=in_specs, out_specs=out_specs, check_vma=False
    )
```

profile of v0, /device:TPU:65, one launch (start us, length us, event | category | flops | bytes accessed | tf_op | source)
XLA Modules:
  0.0 32.2 jit_solution(11436081006270502681)
XLA Ops:
  0.6 1.1 %pack_y.1 = (f32[29,8,128]{2,1,0:T(8,128)S(1)}, f32[29,8,128]{2,1,0:T(8,128)S(1)}, f32[3,8,16,128]{3,2,1,0:T(8,128)S(1)}, f32[3,8,16,128]{3,2,1,0:T(8,128)S(1)},...) custom-call(s32[16]{0:T(128)} %seg_y_hbm.1, s32[8]{0:T(128)} %seg_z_hbm.1, s32[128]{0:T(128)} %seg_x_hbm.1, ...), custom_call_target="tpu_custom_call" | custom-call | tf_op jit(solution)/shard_map/pack_y/pallas_call | solution.py:491
  1.8 1.9 %collective-permute-start = (f32[29,8,128]{2,1,0:T(8,128)S(1)}, f32[29,8,128]{2,1,0:T(8,128)S(1)}, u32[]{:S(2)}, u32[]{:S(2)}) collective-permute-start(f32[29,8,128]{2,1,0:T(8,128)S(1)} %get-tuple-element.20), channel_id=1, source_target_pairs={{0,1},{2,3},{4,5},{6,7},{8,9},{10,11},{1,0},{3,2},{5,4},{7,6},{9,8... | collective-permute-start | bytes 356360 | tf_op jit(solution)/shard_map/ppermute | solution.py:482
  3.7 6.1 %collective-permute-start.1 = (f32[29,8,128]{2,1,0:T(8,128)S(1)}, f32[29,8,128]{2,1,0:T(8,128)S(1)}, u32[]{:S(2)}, u32[]{:S(2)}) collective-permute-start(f32[29,8,128]{2,1,0:T(8,128)S(1)} %get-tuple-element.21), channel_id=1, source_target_pairs={{1,2},{3,4},{5,6},{7,8},{9,10},{2,1},{4,3},{6,5},{8,7},{10,9},{13,... | collective-permute-start | bytes 356360 | tf_op jit(solution)/shard_map/ppermute | solution.py:482
  9.8 0.0 collective-permute-done.y_first
  9.8 2.2 %collective-permute-done.1.y_second = f32[29,8,128]{2,1,0:T(8,128)S(1)} collective-permute-done((f32[29,8,128]{2,1,0:T(8,128)S(1)}, f32[29,8,128]{2,1,0:T(8,128)S(1)}, u32[]{:S(2)}, u32[]{:S(2)}) %collective-permute-start.1) | collective-permute-done | bytes 118816 | tf_op jit(solution)/shard_map/ppermute | solution.py:482
  12.0 0.1 pack_z.1
  12.1 9.6 %collective-permute-start.2 = (f32[25,24,128]{2,1,0:T(8,128)S(1)}, f32[25,24,128]{2,1,0:T(8,128)S(1)}, u32[]{:S(2)}, u32[]{:S(2)}) collective-permute-start(f32[25,24,128]{2,1,0:T(8,128)S(1)} %get-tuple-element.25), channel_id=1, source_target_pairs={{0,12},{24,36},{48,60},{72,84},{96,108},{120,132},{144,156},{168,1... | collective-permute-start | bytes 921608 | tf_op jit(solution)/shard_map/ppermute | solution.py:482
  21.7 1.9 %collective-permute-start.3 = (f32[25,24,128]{2,1,0:T(8,128)S(1)}, f32[25,24,128]{2,1,0:T(8,128)S(1)}, u32[]{:S(2)}, u32[]{:S(2)}) collective-permute-start(f32[25,24,128]{2,1,0:T(8,128)S(1)} %get-tuple-element.26), channel_id=1, source_target_pairs={{12,24},{36,48},{60,72},{84,96},{108,120},{132,144},{156,168},{180... | collective-permute-start | bytes 921608 | tf_op jit(solution)/shard_map/ppermute | solution.py:482
  23.6 1.8 %solve_inner.1 = (f32[3,8,24,128]{3,2,1,0:T(8,128)S(1)}, f32[3,8,24,128]{3,2,1,0:T(8,128)S(1)}, f32[8,24,128]{2,1,0:T(8,128)S(1)}, f32[6,8,24,128]{3,2,1,0:T(8,1...) custom-call(f32[3,8,16,128]{3,2,1,0:T(8,128)S(1)} %get-tuple-element.22.field, ...), custom_call_target="tpu_custom_call" | custom-call | tf_op jit(solution)/shard_map/solve_inner/pallas_call | solution.py:521
  25.4 0.0 collective-permute-done.2.z_first
  25.4 1.1 %solve_near.1 = (f32[3,2,16,128]{3,2,1,0:T(8,128)S(1)}, f32[3,4,24,128]{3,2,1,0:T(8,128)S(1)}) custom-call(f32[25,24,128]{2,1,0:T(8,128)S(1)} %collective-permute-done.2.z_first, f32[3,8,24,128]{3,2,1,0:T(8,128)S(1)} %get-tuple-element.27.refs_0_, f32[3,8,24,128]{3,2,1,0:T(8,128)S(1)} %get-tuple-element.28.refs_1_, ...), custom_call_target="tpu_custom_call" | custom-call | tf_op jit(solution)/shard_map/solve_near/pallas_call | solution.py:529
  26.6 3.3 %collective-permute-done.3.z_second = f32[25,24,128]{2,1,0:T(8,128)S(1)} collective-permute-done((f32[25,24,128]{2,1,0:T(8,128)S(1)}, f32[25,24,128]{2,1,0:T(8,128)S(1)}, u32[]{:S(2)}, u32[]{:S(2)}) %collective-permute-start.3) | collective-permute-done | bytes 307232 | tf_op jit(solution)/shard_map/ppermute | solution.py:482
  29.9 2.3 %solve_far.1 = (f32[3,8,16,128]{3,2,1,0:T(8,128)}, f32[6,2,128]{2,1,0:T(2,128)}) custom-call(f32[8,128]{1,0:T(8,128)S(1)} %get-tuple-element.19.labels, f32[29,8,128]{2,1,0:T(8,128)S(1)} %collective-permute-done.y_first, f32[29,8,128]{2,1,0:T(8,128)S(1)} %collective-permute-done.1.y_second, f32[25,24,128]{2,1,0:T(8,128)S(1)} %collective-permute-done.2.z_first, ...), custom_call_target="tpu_custom_call" | custom-call | tf_op jit(solution)/shard_map/solve_far/pallas_call | solution.py:538
Async XLA Ops:
  1.8 8.0 %collective-permute-start = (f32[29,8,128]{2,1,0:T(8,128)S(1)}, f32[29,8,128]{2,1,0:T(8,128)S(1)}, u32[]{:S(2)}, u32[]{:S(2)}) collective-permute-start(f32[29,8,128]{2,1,0:T(8,128)S(1)} %get-tuple-element.20), channel_id=1, source_target_pairs={{0,1},{2,3},{4,5},{6,7},{8,9},{10,11},{1,0},{3,2},{5,4},{7,6},{9,8... | collective-permute-start | bytes 356360 | tf_op jit(solution)/shard_map/ppermute | solution.py:482
  3.7 8.3 %collective-permute-start.1 = (f32[29,8,128]{2,1,0:T(8,128)S(1)}, f32[29,8,128]{2,1,0:T(8,128)S(1)}, u32[]{:S(2)}, u32[]{:S(2)}) collective-permute-start(f32[29,8,128]{2,1,0:T(8,128)S(1)} %get-tuple-element.21), channel_id=1, source_target_pairs={{1,2},{3,4},{5,6},{7,8},{9,10},{2,1},{4,3},{6,5},{8,7},{10,9},{13,... | collective-permute-start | bytes 356360 | tf_op jit(solution)/shard_map/ppermute | solution.py:482
  12.1 13.4 %collective-permute-start.2 = (f32[25,24,128]{2,1,0:T(8,128)S(1)}, f32[25,24,128]{2,1,0:T(8,128)S(1)}, u32[]{:S(2)}, u32[]{:S(2)}) collective-permute-start(f32[25,24,128]{2,1,0:T(8,128)S(1)} %get-tuple-element.25), channel_id=1, source_target_pairs={{0,12},{24,36},{48,60},{72,84},{96,108},{120,132},{144,156},{168,1... | collective-permute-start | bytes 921608 | tf_op jit(solution)/shard_map/ppermute | solution.py:482
  21.7 8.2 %collective-permute-start.3 = (f32[25,24,128]{2,1,0:T(8,128)S(1)}, f32[25,24,128]{2,1,0:T(8,128)S(1)}, u32[]{:S(2)}, u32[]{:S(2)}) collective-permute-start(f32[25,24,128]{2,1,0:T(8,128)S(1)} %get-tuple-element.26), channel_id=1, source_target_pairs={{12,24},{36,48},{60,72},{84,96},{108,120},{132,144},{156,168},{180... | collective-permute-start | bytes 921608 | tf_op jit(solution)/shard_map/ppermute | solution.py:482
where the time goes:
time: 32.4 us; the launch traced here: 32.2 us
  starting transfers between devices  19.6 us (60%)
  Pallas kernels  6.44 us (20%)
  waiting for transfers between devices  5.53 us (17%)
  between operations  0.69 us (2%)
    ppermute x4, starting transfers between devices, exchange(): lax.ppermute(block, axis, pairs + [(j, i) for i, j in pairs])  19.6 us
    ppermute x4, waiting for transfers between devices, exchange(): lax.ppermute(block, axis, pairs + [(j, i) for i, j in pairs])  5.53 us
    pallas_call x1, Pallas kernels, on_device(): pl.pallas_call(solve_far, out_shape=(f32(3, DEPTH, ROWS, WIDTH), f32(6, S...  2.34 us
    pallas_call x1, Pallas kernels, on_device(): pl.pallas_call(solve_inner, out_shape=[f32(*size) for size in sizes(DEPTH...  1.78 us
    pallas_call x1, Pallas kernels, on_device(): pl.pallas_call(solve_near, out_shape=(f32(3, 2, ROWS, WIDTH), f32(3, 4, T...  1.13 us
    pallas_call x1, Pallas kernels, on_device(): pl.pallas_call(pack_y, out_shape=[f32(PAIRS + 1, 8, WIDTH)] * 2 + blocks...  1.13 us
  transfers between devices with their start and end apart: 4, of which 2 were waited for; matrix products, arithmetic and copies ran while one was open for 0% of the time, Pallas kernels for 9%

commit v1 on v0

v1 whole, which is shorter than its diff:
```python
import functools

import jax
import jax.numpy as jnp
from jax import lax
from jax.experimental import pallas as pl
from jax.experimental.pallas import tpu as pltpu
from jax.sharding import PartitionSpec as P


SX = 32
SY = 4
SZ = 2
DEPTH = 8
ROWS = 16
WIDTH = 128
TALL = 24
DAMPING = 0.6

POISSON = 0.3
LAME = POISSON / ((1.0 + POISSON) * (1.0 - 2.0 * POISSON))
SHEAR = 0.5 / (1.0 + POISSON)

FIELD, LOAD, MODULUS = 0, 1, 2
UP_ROWS, DOWN_ROWS = (3, 2, 3), (4, 3, 3)
UP_AT, DOWN_AT = (0, 72, 120), (0, 96, 168)
UP_SIZE, DOWN_SIZE = 144, 192
UP_PLANES = (
    [(FIELD, c, z) for c in range(3) for z in (5, 6, 7)]
    + [(LOAD, c, z) for c in range(3) for z in (6, 7)]
    + [(MODULUS, 0, z) for z in (5, 6, 7)]
)
DOWN_PLANES = (
    [(FIELD, c, z) for c in range(3) for z in (0, 1, 2, 3)]
    + [(LOAD, c, z) for c in range(3) for z in (0, 1, 2)]
    + [(MODULUS, 0, z) for z in (0, 1, 2)]
)


LABEL_PLANE = (MODULUS, 0, 0)


def y_rows(kind, c, z, up):
    rows, start = (UP_ROWS[kind], UP_AT[kind]) if up else (DOWN_ROWS[kind], DOWN_AT[kind])
    start += rows * (DEPTH * c + z)
    return slice(start, start + rows)


def is_even(axis):
    return lax.axis_index(axis) % 2 == 0


def pack_y(
    seg_y_hbm, seg_z_hbm, seg_x_hbm, field_hbm, load_hbm, modulus_hbm,
    up, down, field, load, modulus, labels, seg_y, seg_z, seg_x, sems,
):
    pairs = (
        (field_hbm, field), (load_hbm, load), (modulus_hbm, modulus),
        (seg_y_hbm, seg_y), (seg_z_hbm, seg_z), (seg_x_hbm, seg_x),
    )
    copies = [pltpu.make_async_copy(src, dst, sems.at[k]) for k, (src, dst) in enumerate(pairs)]
    for copy in copies:
        copy.start()
    for copy, ref, kind in zip(copies, (field, load, modulus), (FIELD, LOAD, MODULUS)):
        copy.wait()
        for c in range(1 if kind == MODULUS else 3):
            for z in range(DEPTH):
                at = (z,) if kind == MODULUS else (c, z)
                up[y_rows(kind, c, z, True), :] = ref[(*at, slice(ROWS - UP_ROWS[kind], ROWS), slice(None))]
                down[y_rows(kind, c, z, False), :] = ref[(*at, slice(0, DOWN_ROWS[kind]), slice(None))]
    for copy in copies[3:]:
        copy.wait()
    down[DOWN_SIZE:, :] = jnp.full((8, WIDTH), seg_y[0].astype(jnp.float32))
    for k in range(SY):
        labels[k : k + 1, :] = jnp.full((1, WIDTH), seg_y[4 * k].astype(jnp.float32))
    for k in range(SZ):
        labels[SY + k : SY + k + 1, :] = jnp.full((1, WIDTH), seg_z[4 * k].astype(jnp.float32))
    labels[7:8, :] = seg_x[...].reshape(1, WIDTH).astype(jnp.float32)


def edge_tile(below, above, kind, c, z):
    parts = [above[y_rows(kind, c, z, False), :]]
    spare = 8 - UP_ROWS[kind] - DOWN_ROWS[kind]
    parts.append(jnp.zeros((spare, WIDTH), jnp.float32))
    parts.append(below[y_rows(kind, c, z, True), :])
    return jnp.concatenate(parts, axis=0)


def pack_z(labels, field, load, modulus, y_below, y_above, first, second):
    even = is_even("slab")
    lane = lax.broadcasted_iota(jnp.int32, (TALL, WIDTH), 1)
    tall = {}

    def whole(kind, c, z):
        if (kind, c, z) not in tall:
            own = (field if kind == FIELD else load)[c, z] if kind != MODULUS else modulus[z]
            tall[kind, c, z] = jnp.concatenate(
                [own, edge_tile(y_below, y_above, kind, c, z)], axis=0
            )
        return tall[kind, c, z]

    for index, plane in enumerate(DOWN_PLANES):
        down = whole(*plane)
        if plane == LABEL_PLANE:
            down = jnp.where(lane == WIDTH - 1, labels[SY : SY + 1, :], down)
        up = whole(*UP_PLANES[index]) if index < len(UP_PLANES) else down
        first[index] = jnp.where(even, up, down)
        second[index] = jnp.where(even, down, up)


def roll_x(value, shift):
    return pltpu.roll(value, shift % WIDTH, 1)


def roll_y(value, shift):
    return pltpu.roll(value, shift % TALL, 0)


class Planes:
    def __init__(self, mine, offset, given=None):
        self.mine, self.offset, self.given = mine, offset, given
        self.written = set()

    def where(self, lead, z, tile, ref, offset):
        rows = slice(None) if tile is None else slice(8 * tile, 8 * tile + 8)
        return ref, (*lead, z + offset, rows, slice(None))

    def load(self, *lead, z, tile=None):
        own = {(*lead, z, t) in self.written for t in (range(3) if tile is None else (tile,))}
        assert len(own) == 1
        if own.pop():
            ref, at = self.where(lead, z, tile, self.mine, self.offset)
        else:
            ref, at = self.where(lead, z, tile, self.given, 0)
        return ref[at]

    def store(self, value, *lead, z, tile=None):
        self.written |= {(*lead, z, t) for t in (range(3) if tile is None else (tile,))}
        ref, at = self.where(lead, z, tile, self.mine, self.offset)
        ref[at] = value


def fill(state, planes, own_block=None, z_part=None):
    work, loads, elem = state[:3]
    slab_pos, sub_pos = lax.axis_index("slab"), lax.axis_index("sub")
    last_slab, last_sub = lax.axis_size("slab") - 1, lax.axis_size("sub") - 1

    def gather(kind, c, z):
        if z < 0:
            return z_part[UP_PLANES.index((kind, c, z + DEPTH))]
        if z >= DEPTH:
            return z_part[DOWN_PLANES.index((kind, c, z - DEPTH))]
        field, load, modulus, y_below, y_above = own_block
        own = (field if kind == FIELD else load)[c, z] if kind != MODULUS else modulus[z]
        return jnp.concatenate([own, edge_tile(y_below, y_above, kind, c, z)], axis=0)

    row = lax.broadcasted_iota(jnp.int32, (TALL, WIDTH), 0)
    lane = lax.broadcasted_iota(jnp.int32, (TALL, WIDTH), 1)
    inside = (lane < WIDTH - 1) & ((row != ROWS - 1) | (sub_pos != last_sub))
    inside_top = inside & (slab_pos != last_slab)
    for z in planes:
        if -3 <= z <= 10:
            value = gather(MODULUS, 0, z)
            elem.store(jnp.where(inside_top if z == DEPTH - 1 else inside, value, 0.0), z=z)
        for c in range(3):
            work.store(gather(FIELD, c, z), c, z=z)
            if -2 <= z <= 10:
                loads.store(gather(LOAD, c, z), c, z=z)


def invert(state, first, last):
    elem, inv = state[2], state[3]
    diag_scale = (LAME + 4.0 * SHEAR) / 9.0
    off_scale = (LAME + SHEAR) / 12.0
    before = None
    for z in range(first - 1, last + 1):
        e = elem.load(z=z)
        right = roll_x(e, 1)
        sum_x, dif_x = e + right, right - e
        sum_up, dif_up = roll_y(sum_x, 1), roll_y(dif_x, 1)
        now = (sum_up + sum_x, sum_up - sum_x, dif_up + dif_x, dif_up - dif_x)
        if before is not None:
            p = diag_scale * (before[0] + now[0])
            cc = off_scale * (before[1] - now[1])
            b = off_scale * (before[2] - now[2])
            a = off_scale * (before[3] + now[3])
            pp = p * p
            co00, co11, co22 = pp - cc * cc, pp - b * b, pp - a * a
            co01, co02, co12 = b * cc - a * p, a * cc - b * p, a * b - p * cc
            det = p * co00 + a * co01 + b * co02
            scale = jnp.where(det != 0.0, DAMPING / det, 0.0)
            for k, value in enumerate((co00, co01, co02, co11, co12, co22)):
                inv.store(value * scale, k, z=z)
        before = now


def spread(state, planes):
    work, modes = state[0], state[4]
    for c in range(3):
        for z in planes:
            v = work.load(c, z=z)
            left = roll_x(v, -1)
            sum_x, dif_x = v + left, left - v
            sum_up, dif_up = roll_y(sum_x, -1), roll_y(dif_x, -1)
            modes.store(sum_x + sum_up, 4 * c, z=z)
            modes.store(dif_x + dif_up, 4 * c + 1, z=z)
            modes.store(sum_up - sum_x, 4 * c + 2, z=z)
            modes.store(dif_up - dif_x, 4 * c + 3, z=z)


def stress(state, lo, hi, resume=False, join=False):
    elem, modes, forces = state[2], state[4], state[5]
    for tile in range(3):
        old = [modes.load(k, z=lo, tile=tile) for k in range(12)]
        held = [forces.load(k, z=lo, tile=tile) for k in range(12)] if resume else None
        for z in range(lo, hi):
            e = elem.load(z=z, tile=tile)
            new = [modes.load(k, z=z + 1, tile=tile) for k in range(12)]
            total = [None if k % 4 == 0 else new[k] + old[k] for k in range(12)]
            delta = [new[k] - old[k] for k in range(12)]
            xa, xb, xc = total[1], total[2], total[3]
            xd, xe, xf, xg = delta[0], delta[1], delta[2], delta[3]
            ya, yb, yc = total[5], total[6], total[7]
            yd, ye, yf, yg = delta[4], delta[5], delta[6], delta[7]
            za, zb, zc = total[9], total[10], total[11]
            zd, ze, zf, zg = delta[8], delta[9], delta[10], delta[11]
            lam0, mu0 = e * (LAME / 16.0), e * (SHEAR / 16.0)
            lam1, mu1 = e * (LAME / 48.0), e * (SHEAR / 48.0)
            twice = e * (SHEAR / 8.0)
            last_scale = e * ((LAME + 4.0 * SHEAR) / 144.0)
            t = lam0 * (xa + yb + zd)
            xy, xz, yz = mu0 * (xb + ya), mu0 * (xd + za), mu0 * (yd + zb)
            s_x, s_y, s_z = lam1 * (yc + ze), lam1 * (xc + zf), lam1 * (xe + yf)
            q = xf + ye + zc
            even = (
                None, t + twice * xa, xy, s_y + mu0 * xc,
                None, xy, t + twice * yb, s_x + mu0 * yc,
                None, xz, yz, mu1 * (q + zc),
            )
            odd = (
                xz, s_z + mu0 * xe, mu1 * (q + xf), last_scale * xg,
                yz, mu1 * (q + ye), s_z + mu0 * yf, last_scale * yg,
                t + twice * zd, s_x + mu0 * ze, s_y + mu0 * zf, last_scale * zg,
            )
            for k in range(12):
                low = -odd[k] if even[k] is None else even[k] - odd[k]
                forces.store(low if held is None else held[k] + low, k, z=z, tile=tile)
            held = [odd[k] if even[k] is None else even[k] + odd[k] for k in range(12)]
            old = new
        for k in range(12):
            total = forces.load(k, z=hi, tile=tile) + held[k] if join else held[k]
            forces.store(total, k, z=hi, tile=tile)


def misfit(state, z):
    loads, forces = state[1], state[5]
    out = []
    for c in range(3):
        f = [forces.load(4 * c + k, z=z) for k in range(4)]
        sum_x = (f[0] - f[2]) + roll_y(f[0] + f[2], 1)
        dif_x = (f[1] - f[3]) + roll_y(f[1] + f[3], 1)
        out.append(loads.load(c, z=z) - ((sum_x - dif_x) + roll_x(sum_x + dif_x, 1)))
    return out


def relax(state, planes):
    work, inv = state[0], state[3]
    table = ((0, 1, 2), (1, 3, 4), (2, 4, 5))
    for z in planes:
        m = [inv.load(k, z=z) for k in range(6)]
        r = misfit(state, z)
        for c in range(3):
            i, j, k = table[c]
            step = m[i] * r[0] + m[j] * r[1] + m[k] * r[2]
            work.store(work.load(c, z=z) + step, c, z=z)


def solve_inner(even, *refs):
    @pl.when(is_even("slab") == even)
    def mine():
        inner(*refs)


def inner(field, load, modulus, y_below, y_above, *refs):
    state = [Planes(ref, 0) for ref in refs[:6]]
    residual = refs[6]
    fill(state, range(0, 8), own_block=(field, load, modulus, y_below, y_above))
    invert(state, 1, 7)
    spread(state, range(0, 8))
    stress(state, 0, 7)
    relax(state, range(1, 7))
    spread(state, range(1, 7))
    stress(state, 1, 6)
    relax(state, range(2, 6))
    spread(state, range(2, 6))
    stress(state, 2, 5)
    for z in (3, 4):
        for c, value in enumerate(misfit(state, z)):
            residual[c, z - 3] = value


LOWER, UPPER = (0, 1), (6, 7)


def solve_side(lower, z_part, given, mine, smooth, smooth_from):
    state = [Planes(ref, 3, old) for ref, old in zip(mine, given)]
    if lower:
        fill(state, range(-3, 0), z_part=z_part)
        invert(state, -2, 0)
        for first, last in ((-3, 0), (-2, 1), (-1, 2)):
            spread(state, range(first, last))
            stress(state, first, last, join=True)
            if last < 2:
                relax(state, range(first + 1, last + 1))
    else:
        fill(state, range(8, 12), z_part=z_part)
        invert(state, 8, 10)
        for first, last in ((7, 11), (6, 10), (5, 9)):
            spread(state, range(first + 1, last + 1))
            stress(state, first, last, resume=True)
            if last > 9:
                relax(state, range(first, last))
    for k, z in enumerate(LOWER if lower else UPPER):
        for c in range(3):
            smooth[c, smooth_from + k] = state[0].load(c, z=z)[:ROWS]
    return {z: misfit(state, z) for z in ((0, 1, 2) if lower else (5, 6, 7, 8))}


def prepare(labels, chosen):
    target = lax.broadcasted_iota(jnp.int32, (WIDTH, WIDTH), 0) % SX
    hit = jnp.where(target.astype(jnp.float32) == labels[7:8, :], 1.0, 0.0)
    chosen[...] = hit.astype(jnp.bfloat16)


def restrict(kz, residual, labels, chosen, y_label, z_label, rows):
    slab_pos, sub_pos = lax.axis_index("slab"), lax.axis_index("sub")
    last_slab, last_sub = lax.axis_size("slab") - 1, lax.axis_size("sub") - 1
    row = lax.broadcasted_iota(jnp.int32, (TALL, WIDTH), 0)

    def flag(value, segment):
        return jnp.where(value == segment.astype(jnp.float32), 1.0, 0.0)

    start_z = SZ * slab_pos + kz
    low = flag(labels[SY + kz : SY + kz + 1, :], start_z)
    if kz == 0:
        high = flag(labels[SY + 1 : SY + 2, :], start_z)
    else:
        high = jnp.where(slab_pos != last_slab, flag(z_label, start_z), 0.0)
    sums = [None] * 5
    for step in range(5):
        r = residual[4 * kz + step]
        if step in (0, 4):
            r = [(low if step == 0 else high) * value for value in r]
        q = 0.5 * (step - 2)
        terms = [r[0], r[1], r[2], q * r[1], q * r[0]]
        for k in range(5 if q != 0.0 else 3):
            sums[k] = terms[k] if sums[k] is None else sums[k] + terms[k]
    r0, r1, r2, z1, z0 = sums
    count_z, moment_z = low + 3.0 + high, high - low

    start_y = SY * sub_pos
    owns_next = jnp.where(sub_pos != last_sub, flag(y_label, start_y + SY - 1), 0.0)
    lane = lax.broadcasted_iota(jnp.int32, (1, WIDTH), 1)
    group = lane // SX
    seg_x = labels[7:8, :]
    q_x = 0.5 * (lane.astype(jnp.float32) - 4.0 * seg_x - 2.0)
    count_y = jnp.zeros((1, WIDTH), jnp.float32)
    moment_y = jnp.zeros((1, WIDTH), jnp.float32)

    def total(value):
        return jnp.sum(value, axis=0, keepdims=True)

    for ky in range(SY):
        first = flag(labels[ky : ky + 1, :], start_y + ky)
        final = flag(labels[ky + 1 : ky + 2, :], start_y + ky) if ky < SY - 1 else owns_next
        local = row - 4 * ky
        weight = jnp.where((local > 0) & (local < 4), 1.0, 0.0)
        weight = jnp.where(local == 0, first, jnp.where(local == 4, final, weight))
        moment = weight * (0.5 * (local - 2).astype(jnp.float32))
        count_y = jnp.where(group == ky, first + 3.0 + final, count_y)
        moment_y = jnp.where(group == ky, final - first, moment_y)
        plain = [total(weight * value) for value in (r0, r1, r2)]
        turned = [
            total(moment * r2 - weight * z1),
            total(weight * z0) - q_x * plain[2],
            q_x * plain[1] - total(moment * r0),
        ]
        for k, value in enumerate(plain + turned + [jnp.ones((1, WIDTH), jnp.float32), q_x]):
            rows[8 * ky + k : 8 * ky + k + 1, :] = value

    rest, parts = rows[...], []
    for _ in range(3):
        parts.append(rest.astype(jnp.bfloat16))
        rest = rest - parts[-1].astype(jnp.float32)
    totals = lax.dot_general(
        jnp.concatenate(parts, axis=0), chosen[...], (((1,), (1,)), ((), ())),
        preferred_element_type=jnp.float32,
    )
    totals = totals[0:32] + totals[32:64] + totals[64:96]
    s = totals[0:8]
    for ky in range(1, SY):
        s = jnp.where(group == ky, totals[8 * ky : 8 * ky + 8], s)
    s = [s[k : k + 1] for k in range(8)]
    count_x, moment_x = s[6], s[7]
    count = count_x * count_y * count_z
    centre = [
        moment_x * count_y * count_z / count,
        count_x * moment_y * count_z / count,
        count_x * count_y * moment_z / count,
    ]
    scale = 1.0 / jnp.sqrt(count)
    turned = [
        s[3] - (centre[1] * s[2] - centre[2] * s[1]),
        s[4] - (centre[2] * s[0] - centre[0] * s[2]),
        s[5] - (centre[0] * s[1] - centre[1] * s[0]),
    ]
    return [value * scale for value in s[:3] + turned]


def z_label(part):
    row = part[DOWN_PLANES.index(LABEL_PLANE), 0:1, :]
    return jnp.broadcast_to(row[:, WIDTH - 1 :], (1, WIDTH))


def with_middle(residual, middle):
    residual |= {z: [middle[c, z - 3] for c in range(3)] for z in (3, 4)}
    return residual


def solve_near(labels, chosen, y_above, z_first, *refs):
    states, (smooth, coarse), rows, mine = (refs[7:14], refs[:7]), refs[14:16], refs[16], refs[17:23]
    for lower in (False, True):
        *given, middle = states[lower]

        @pl.when(is_even("slab") != lower)
        def side(given=given, middle=middle):
            residual = solve_side(lower, z_first, given, mine, smooth, 0)
            coarse_rows = restrict(
                0 if lower else 1, with_middle(residual, middle), labels, chosen,
                y_above[DOWN_SIZE : DOWN_SIZE + 1, :], z_label(z_first), rows,
            )
            for k in range(6):
                coarse[k : k + 1, :] = coarse_rows[k]


def solve_far(labels, chosen, y_above, z_second, *refs):
    states, (near_smooth, near_coarse) = (refs[:7], refs[7:14]), refs[14:16]
    (smooth, coarse), rows, mine = refs[16:18], refs[18], refs[19:25]

    for lower in (True, False):
        *given, middle = states[lower]

        @pl.when(is_even("slab") == lower)
        def side(given=given, middle=middle):
            near, far, kz = (UPPER, LOWER, 0) if lower else (LOWER, UPPER, 1)
            for c in range(3):
                for z in range(2, 6):
                    smooth[c, z] = given[0][c, z, :ROWS, :]
                for k, z in enumerate(near):
                    smooth[c, z] = near_smooth[c, k]
            residual = solve_side(lower, z_second, given, mine, smooth, far[0])
            coarse_rows = restrict(
                kz, with_middle(residual, middle), labels, chosen,
                y_above[DOWN_SIZE : DOWN_SIZE + 1, :], z_label(z_second), rows,
            )
            for k in range(6):
                coarse[k, kz : kz + 1, :] = coarse_rows[k]
                coarse[k, 1 - kz : 2 - kz, :] = near_coarse[k : k + 1, :]


VMEM = pl.BlockSpec(memory_space=pltpu.VMEM)


def f32(*shape):
    return jax.ShapeDtypeStruct(shape, jnp.float32)


def scratch(*shape):
    return pltpu.VMEM(shape, jnp.float32)


def on_device(field_init, load, modulus, seg_z, seg_y, seg_x):
    def swap(block, axis, start):
        pairs = [(i, i + 1) for i in range(start, lax.axis_size(axis) - 1, 2)]
        return lax.ppermute(block, axis, pairs + [(j, i) for i, j in pairs])

    def limit(mib):
        return pltpu.CompilerParams(vmem_limit_bytes=mib << 20)

    hbm = pl.BlockSpec(memory_space=pltpu.MemorySpace.HBM)
    blocks = [f32(3, DEPTH, ROWS, WIDTH), f32(3, DEPTH, ROWS, WIDTH), f32(DEPTH, ROWS, WIDTH)]
    arguments = (seg_y, seg_z, seg_x, field_init, load, modulus)
    up, down, field_init, load, modulus, labels = pl.pallas_call(
        pack_y,
        out_shape=[f32(UP_SIZE, WIDTH), f32(DOWN_SIZE + 8, WIDTH)] + blocks + [f32(8, WIDTH)],
        in_specs=[hbm] * 6,
        out_specs=[VMEM] * 6,
        scratch_shapes=[
            pltpu.SMEM((ROWS,), jnp.int32),
            pltpu.SMEM((DEPTH,), jnp.int32),
            pltpu.VMEM((WIDTH,), jnp.int32),
            pltpu.SemaphoreType.DMA((6,)),
        ],
        compiler_params=limit(4),
        name="pack_y",
    )(*[pltpu.with_memory_space_constraint(value, pltpu.MemorySpace.HBM) for value in arguments])
    steps = [(i, i + 1) for i in range(lax.axis_size("sub") - 1)]
    y_above = lax.ppermute(down, "sub", [(j, i) for i, j in steps])
    y_below = lax.ppermute(up, "sub", steps)
    y_parts = (y_below, y_above)
    chosen = pl.pallas_call(
        prepare,
        out_shape=jax.ShapeDtypeStruct((WIDTH, WIDTH), jnp.bfloat16),
        in_specs=[VMEM],
        out_specs=VMEM,
        compiler_params=limit(1),
        name="prepare",
    )(labels)
    first, second = pl.pallas_call(
        pack_z,
        out_shape=(f32(len(DOWN_PLANES), TALL, WIDTH),) * 2,
        in_specs=[VMEM] * 6,
        out_specs=(VMEM, VMEM),
        compiler_params=limit(4),
        name="pack_z",
    )(labels, field_init, load, modulus, *y_parts)
    z_second = swap(second, "slab", 1)
    z_first = swap(first, "slab", 0)

    def sizes(planes):
        return [(3, planes, TALL, WIDTH)] * 2 + [(planes, TALL, WIDTH)] + [
            (n, planes, TALL, WIDTH) for n in (6, 12, 12)
        ]

    states = []
    for even in (False, True):
        states += pl.pallas_call(
            functools.partial(solve_inner, even),
            out_shape=[f32(*size) for size in sizes(DEPTH)] + [f32(3, 2, TALL, WIDTH)],
            in_specs=[VMEM] * 5,
            out_specs=[VMEM] * 7,
            compiler_params=limit(6),
        )(field_init, load, modulus, *y_parts)
    near = pl.pallas_call(
        solve_near,
        out_shape=(f32(3, 2, ROWS, WIDTH), f32(8, WIDTH)),
        in_specs=[VMEM] * 18,
        out_specs=(VMEM, VMEM),
        scratch_shapes=[scratch(8 * SY, WIDTH)] + [scratch(*size) for size in sizes(15)],
        compiler_params=limit(12),
        name="solve_near",
    )(labels, chosen, y_above, z_first, *states)
    return pl.pallas_call(
        solve_far,
        out_shape=(f32(3, DEPTH, ROWS, WIDTH), f32(6, SZ, SY * SX)),
        in_specs=[VMEM] * 20,
        out_specs=(VMEM, VMEM),
        scratch_shapes=[scratch(8 * SY, WIDTH)] + [scratch(*size) for size in sizes(15)],
        compiler_params=limit(14),
        name="solve_far",
    )(labels, chosen, y_above, z_second, *states, *near)


def solution(mesh):
    in_specs = (
        P(None, "slab", "sub", None),
        P(None, "slab", "sub", None),
        P("slab", "sub", None),
        P("slab"),
        P("sub"),
        P(),
    )
    out_specs = (P(None, "slab", "sub", None), P(None, "slab", "sub"))
    return jax.shard_map(
        on_device, mesh=mesh, in_specs=in_specs, out_specs=out_specs, check_vma=False
    )
```

time: 32.4 us -> 32.5 us (level)
  the two profiles are of different devices: /device:TPU:65 before, /device:TPU:1 now
where the time goes in v1:
time: 32.5 us; the launch traced here: 32.3 us
  starting transfers between devices  20.7 us (64%)
  Pallas kernels  6.54 us (20%)
  waiting for transfers between devices  4.32 us (13%)
  between operations  0.7 us (2%)
    ppermute x2, starting transfers between devices, swap(): return lax.ppermute(block, axis, pairs + [(j, i) for i, j in pairs])  14 us
    ppermute x1, starting transfers between devices, on_device(): y_below = lax.ppermute(up, 'sub', steps)  5.45 us
    ppermute x2, waiting for transfers between devices, swap(): return lax.ppermute(block, axis, pairs + [(j, i) for i, j in pairs])  2.93 us
    pallas_call x1, Pallas kernels, on_device(): pl.pallas_call(solve_far, out_shape=(f32(3, DEPTH, ROWS, WIDTH), f32(6, S...  2.19 us
    pallas_call x2, Pallas kernels, on_device(): pl.pallas_call(functools.partial(solve_inner, even), out_shape=[f32(*size...  1.81 us
    ppermute x1, waiting for transfers between devices, on_device(): y_below = lax.ppermute(up, 'sub', steps)  1.39 us
    pallas_call x1, Pallas kernels, on_device(): pl.pallas_call(solve_near, out_shape=(f32(3, 2, ROWS, WIDTH), f32(8, WIDT...  1.34 us
    ppermute x1, starting transfers between devices, on_device(): y_above = lax.ppermute(down, 'sub', [(j, i) for i, j in steps])  1.29 us
  transfers between devices with their start and end apart: 4, of which 2 were waited for; matrix products, arithmetic and copies ran while one was open for 0% of the time, Pallas kernels for 10%

profile of v1, /device:TPU:1, one launch (start us, length us, event | category | flops | bytes accessed | tf_op | source)
XLA Modules:
  0.0 32.3 jit_solution(17950396136028929645)
XLA Ops:
  0.6 1.1 %pack_y.1 = (f32[144,128]{1,0:T(8,128)S(1)}, f32[200,128]{1,0:T(8,128)S(1)}, f32[3,8,16,128]{3,2,1,0:T(8,128)S(1)}, f32[3,8,16,128]{3,2,1,0:T(8,128)S(1)}, f32[8...) custom-call(s32[16]{0:T(128)} %seg_y_hbm.1, s32[8]{0:T(128)} %seg_z_hbm.1, s32[128]{0:T(128)} %seg_x_hbm.1, ...), custom_call_target="tpu_custom_call" | custom-call | tf_op jit(solution)/shard_map/pack_y/pallas_call | solution.py:493
  1.8 1.3 %collective-permute-start = (f32[200,128]{1,0:T(8,128)S(1)}, f32[200,128]{1,0:T(8,128)S(1)}, u32[]{:S(2)}, u32[]{:S(2)}) collective-permute-start(f32[200,128]{1,0:T(8,128)S(1)} %get-tuple-element.27), channel_id=1, source_target_pairs={{1,0},{2,1},{3,2},{4,3},{5,4},{6,5},{7,6},{8,7},{9,8},{10,9},{11,1... | collective-permute-start | bytes 307208 | tf_op jit(solution)/shard_map/ppermute | solution.py:508
  3.1 5.4 %collective-permute-start.1 = (f32[144,128]{1,0:T(8,128)S(1)}, f32[144,128]{1,0:T(8,128)S(1)}, u32[]{:S(2)}, u32[]{:S(2)}) collective-permute-start(f32[144,128]{1,0:T(8,128)S(1)} %get-tuple-element.31), channel_id=1, source_target_pairs={{0,1},{1,2},{2,3},{3,4},{4,5},{5,6},{6,7},{7,8},{8,9},{9,10},{10,1... | collective-permute-start | bytes 221192 | tf_op jit(solution)/shard_map/ppermute | solution.py:509
  8.5 1.4 %collective-permute-done.1.y_below.refs_3_ = f32[144,128]{1,0:T(8,128)S(1)} collective-permute-done((f32[144,128]{1,0:T(8,128)S(1)}, f32[144,128]{1,0:T(8,128)S(1)}, u32[]{:S(2)}, u32[]{:S(2)}) %collective-permute-start.1) | collective-permute-done | bytes 73760 | tf_op jit(solution)/shard_map/ppermute | solution.py:509
  9.9 0.0 collective-permute-done.y_above.refs_4_
  9.9 0.1 pack_z.1
  10.0 12.1 %collective-permute-start.3 = (f32[24,24,128]{2,1,0:T(8,128)S(1)}, f32[24,24,128]{2,1,0:T(8,128)S(1)}, u32[]{:S(2)}, u32[]{:S(2)}) collective-permute-start(f32[24,24,128]{2,1,0:T(8,128)S(1)} %get-tuple-element.47), channel_id=1, source_target_pairs={{0,12},{24,36},{48,60},{72,84},{96,108},{120,132},{144,156},{168,1... | collective-permute-start | bytes 884744 | tf_op jit(solution)/shard_map/ppermute | solution.py:485
  22.0 1.9 %collective-permute-start.2 = (f32[24,24,128]{2,1,0:T(8,128)S(1)}, f32[24,24,128]{2,1,0:T(8,128)S(1)}, u32[]{:S(2)}, u32[]{:S(2)}) collective-permute-start(f32[24,24,128]{2,1,0:T(8,128)S(1)} %get-tuple-element.32), channel_id=1, source_target_pairs={{12,24},{36,48},{60,72},{84,96},{108,120},{132,144},{156,168},{180... | collective-permute-start | bytes 884744 | tf_op jit(solution)/shard_map/ppermute | solution.py:485
  24.0 1.8 %shard_map.77 = (f32[3,8,24,128]{3,2,1,0:T(8,128)S(1)}, f32[3,8,24,128]{3,2,1,0:T(8,128)S(1)}, f32[8,24,128]{2,1,0:T(8,128)S(1)}, f32[6,8,24,128]{3,2,1,0:T(8,12...) custom-call(f32[3,8,16,128]{3,2,1,0:T(8,128)S(1)} %get-tuple-element.28.field., ...), custom_call_target="tpu_custom_call" | custom-call | tf_op jit(solution)/shard_map/pallas_call | solution.py:537
  25.8 0.0 collective-permute-done.3.z_first
  25.8 1.3 %solve_near.1 = (f32[3,2,16,128]{3,2,1,0:T(8,128)S(1)}, f32[8,128]{1,0:T(8,128)S(1)}) custom-call(f32[8,128]{1,0:T(8,128)S(1)} %get-tuple-element.26.labels, bf16[128,128]{1,0:T(8,128)(2,1)S(1)} %prepare.1.chosen, f32[200,128]{1,0:T(8,128)S(1)} %collective-permute-done.y_above.refs_4_, f32[24,24,128]{2,1,0:T(8,128)S(1)} %collective-permute-done.3.z_first, ...), custom_call_target="tpu_custom_call" | custom-call | tf_op jit(solution)/shard_map/solve_near/pallas_call | solution.py:544
  27.2 2.9 %collective-permute-done.2.z_second = f32[24,24,128]{2,1,0:T(8,128)S(1)} collective-permute-done((f32[24,24,128]{2,1,0:T(8,128)S(1)}, f32[24,24,128]{2,1,0:T(8,128)S(1)}, u32[]{:S(2)}, u32[]{:S(2)}) %collective-permute-start.2) | collective-permute-done | bytes 294944 | tf_op jit(solution)/shard_map/ppermute | solution.py:485
  30.1 2.2 %solve_far.1 = (f32[3,8,16,128]{3,2,1,0:T(8,128)}, f32[6,2,128]{2,1,0:T(2,128)}) custom-call(f32[8,128]{1,0:T(8,128)S(1)} %get-tuple-element.26.labels, bf16[128,128]{1,0:T(8,128)(2,1)S(1)} %prepare.1.chosen, f32[200,128]{1,0:T(8,128)S(1)} %collective-permute-done.y_above.refs_4_, f32[24,24,128]{2,1,0:T(8,128)S(1)} %collective-permute-done.2.z_second, ...), custom_call_target="tpu_custom_call" | custom-call | tf_op jit(solution)/shard_map/solve_far/pallas_call | solution.py:553
  (2 shorter events, 0.0 us)
Async XLA Ops:
  1.8 8.1 %collective-permute-start = (f32[200,128]{1,0:T(8,128)S(1)}, f32[200,128]{1,0:T(8,128)S(1)}, u32[]{:S(2)}, u32[]{:S(2)}) collective-permute-start(f32[200,128]{1,0:T(8,128)S(1)} %get-tuple-element.27), channel_id=1, source_target_pairs={{1,0},{2,1},{3,2},{4,3},{5,4},{6,5},{7,6},{8,7},{9,8},{10,9},{11,1... | collective-permute-start | bytes 307208 | tf_op jit(solution)/shard_map/ppermute | solution.py:508
  3.1 6.8 %collective-permute-start.1 = (f32[144,128]{1,0:T(8,128)S(1)}, f32[144,128]{1,0:T(8,128)S(1)}, u32[]{:S(2)}, u32[]{:S(2)}) collective-permute-start(f32[144,128]{1,0:T(8,128)S(1)} %get-tuple-element.31), channel_id=1, source_target_pairs={{0,1},{1,2},{2,3},{3,4},{4,5},{5,6},{6,7},{7,8},{8,9},{9,10},{10,1... | collective-permute-start | bytes 221192 | tf_op jit(solution)/shard_map/ppermute | solution.py:509
  10.0 15.8 %collective-permute-start.3 = (f32[24,24,128]{2,1,0:T(8,128)S(1)}, f32[24,24,128]{2,1,0:T(8,128)S(1)}, u32[]{:S(2)}, u32[]{:S(2)}) collective-permute-start(f32[24,24,128]{2,1,0:T(8,128)S(1)} %get-tuple-element.47), channel_id=1, source_target_pairs={{0,12},{24,36},{48,60},{72,84},{96,108},{120,132},{144,156},{168,1... | collective-permute-start | bytes 884744 | tf_op jit(solution)/shard_map/ppermute | solution.py:485
  22.0 8.0 %collective-permute-start.2 = (f32[24,24,128]{2,1,0:T(8,128)S(1)}, f32[24,24,128]{2,1,0:T(8,128)S(1)}, u32[]{:S(2)}, u32[]{:S(2)}) collective-permute-start(f32[24,24,128]{2,1,0:T(8,128)S(1)} %get-tuple-element.32), channel_id=1, source_target_pairs={{12,24},{36,48},{60,72},{84,96},{108,120},{132,144},{156,168},{180... | collective-permute-start | bytes 884744 | tf_op jit(solution)/shard_map/ppermute | solution.py:485

commit v2 on v1

--- a/solution.py
+++ b/solution.py
@@ -24,7 +24,7 @@
 FIELD, LOAD, MODULUS = 0, 1, 2
 UP_ROWS, DOWN_ROWS = (3, 2, 3), (4, 3, 3)
 UP_AT, DOWN_AT = (0, 72, 120), (0, 96, 168)
-UP_SIZE, DOWN_SIZE = 144, 192
+DOWN_SIZE = 192
 UP_PLANES = (
     [(FIELD, c, z) for c in range(3) for z in (5, 6, 7)]
     + [(LOAD, c, z) for c in range(3) for z in (6, 7)]
@@ -52,25 +52,29 @@
 
 def pack_y(
     seg_y_hbm, seg_z_hbm, seg_x_hbm, field_hbm, load_hbm, modulus_hbm,
-    up, down, field, load, modulus, labels, seg_y, seg_z, seg_x, sems,
+    first, second, field, load, modulus, labels, up, down, seg_y, seg_z, seg_x, sems,
 ):
-    pairs = (
-        (field_hbm, field), (load_hbm, load), (modulus_hbm, modulus),
-        (seg_y_hbm, seg_y), (seg_z_hbm, seg_z), (seg_x_hbm, seg_x),
-    )
+    pairs = [(field_hbm.at[c], field.at[c]) for c in range(3)]
+    pairs += [(load_hbm.at[c], load.at[c]) for c in range(3)]
+    pairs += [
+        (modulus_hbm, modulus), (seg_y_hbm, seg_y), (seg_z_hbm, seg_z), (seg_x_hbm, seg_x),
+    ]
     copies = [pltpu.make_async_copy(src, dst, sems.at[k]) for k, (src, dst) in enumerate(pairs)]
     for copy in copies:
         copy.start()
-    for copy, ref, kind in zip(copies, (field, load, modulus), (FIELD, LOAD, MODULUS)):
-        copy.wait()
+    for ref, kind in ((field, FIELD), (load, LOAD), (modulus, MODULUS)):
         for c in range(1 if kind == MODULUS else 3):
+            copies[3 * kind + c].wait()
             for z in range(DEPTH):
                 at = (z,) if kind == MODULUS else (c, z)
                 up[y_rows(kind, c, z, True), :] = ref[(*at, slice(ROWS - UP_ROWS[kind], ROWS), slice(None))]
                 down[y_rows(kind, c, z, False), :] = ref[(*at, slice(0, DOWN_ROWS[kind]), slice(None))]
-    for copy in copies[3:]:
+    for copy in copies[7:]:
         copy.wait()
     down[DOWN_SIZE:, :] = jnp.full((8, WIDTH), seg_y[0].astype(jnp.float32))
+    upward = (lax.axis_index("slab") == 0) & is_even("sub")
+    first[...] = jnp.where(upward, up[...], down[...])
+    second[...] = jnp.where(upward, down[...], up[...])
     for k in range(SY):
         labels[k : k + 1, :] = jnp.full((1, WIDTH), seg_y[4 * k].astype(jnp.float32))
     for k in range(SZ):
@@ -86,7 +90,10 @@
     return jnp.concatenate(parts, axis=0)
 
 
-def pack_z(labels, field, load, modulus, y_below, y_above, first, second):
+def pack_z(labels, field, load, modulus, y_first, y_second, first, second, y_below, y_above):
+    below_first = (lax.axis_index("slab") == 0) & jnp.logical_not(is_even("sub"))
+    y_below[...] = jnp.where(below_first, y_first[...], y_second[...])
+    y_above[...] = jnp.where(below_first, y_second[...], y_first[...])
     even = is_even("slab")
     lane = lax.broadcasted_iota(jnp.int32, (TALL, WIDTH), 1)
     tall = {}
@@ -175,20 +182,20 @@
     before = None
     for z in range(first - 1, last + 1):
         e = elem.load(z=z)
-        right = roll_x(e, 1)
-        sum_x, dif_x = e + right, right - e
-        sum_up, dif_up = roll_y(sum_x, 1), roll_y(dif_x, 1)
-        now = (sum_up + sum_x, sum_up - sum_x, dif_up + dif_x, dif_up - dif_x)
+        up = roll_y(e, 1)
+        sum_y, dif_y = e + up, up - e
+        sum_right, dif_right = roll_x(sum_y, 1), roll_x(dif_y, 1)
+        now = (sum_y + sum_right, dif_y + dif_right, sum_right - sum_y, dif_right - dif_y)
         if before is not None:
-            p = diag_scale * (before[0] + now[0])
-            cc = off_scale * (before[1] - now[1])
-            b = off_scale * (before[2] - now[2])
-            a = off_scale * (before[3] + now[3])
+            p = (diag_scale / off_scale) * (before[0] + now[0])
+            cc = before[1] - now[1]
+            b = before[2] - now[2]
+            a = before[3] + now[3]
             pp = p * p
             co00, co11, co22 = pp - cc * cc, pp - b * b, pp - a * a
             co01, co02, co12 = b * cc - a * p, a * cc - b * p, a * b - p * cc
             det = p * co00 + a * co01 + b * co02
-            scale = jnp.where(det != 0.0, DAMPING / det, 0.0)
+            scale = jnp.where(det != 0.0, (DAMPING / off_scale) / det, 0.0)
             for k, value in enumerate((co00, co01, co02, co11, co12, co22)):
                 inv.store(value * scale, k, z=z)
         before = now
@@ -199,13 +206,13 @@
     for c in range(3):
         for z in planes:
             v = work.load(c, z=z)
-            left = roll_x(v, -1)
-            sum_x, dif_x = v + left, left - v
-            sum_up, dif_up = roll_y(sum_x, -1), roll_y(dif_x, -1)
-            modes.store(sum_x + sum_up, 4 * c, z=z)
-            modes.store(dif_x + dif_up, 4 * c + 1, z=z)
-            modes.store(sum_up - sum_x, 4 * c + 2, z=z)
-            modes.store(dif_up - dif_x, 4 * c + 3, z=z)
+            up = roll_y(v, -1)
+            sum_y, dif_y = v + up, up - v
+            sum_left, dif_left = roll_x(sum_y, -1), roll_x(dif_y, -1)
+            modes.store(sum_y + sum_left, 4 * c, z=z)
+            modes.store(sum_left - sum_y, 4 * c + 1, z=z)
+            modes.store(dif_y + dif_left, 4 * c + 2, z=z)
+            modes.store(dif_left - dif_y, 4 * c + 3, z=z)
 
 
 def stress(state, lo, hi, resume=False, join=False):
@@ -243,8 +250,11 @@
                 t + twice * zd, s_x + mu0 * ze, s_y + mu0 * zf, last_scale * zg,
             )
             for k in range(12):
-                low = -odd[k] if even[k] is None else even[k] - odd[k]
-                forces.store(low if held is None else held[k] + low, k, z=z, tile=tile)
+                if even[k] is None:
+                    low = -odd[k] if held is None else held[k] - odd[k]
+                else:
+                    low = even[k] - odd[k] if held is None else held[k] + (even[k] - odd[k])
+                forces.store(low, k, z=z, tile=tile)
             held = [odd[k] if even[k] is None else even[k] + odd[k] for k in range(12)]
             old = new
         for k in range(12):
@@ -257,9 +267,9 @@
     out = []
     for c in range(3):
         f = [forces.load(4 * c + k, z=z) for k in range(4)]
-        sum_x = (f[0] - f[2]) + roll_y(f[0] + f[2], 1)
-        dif_x = (f[1] - f[3]) + roll_y(f[1] + f[3], 1)
-        out.append(loads.load(c, z=z) - ((sum_x - dif_x) + roll_x(sum_x + dif_x, 1)))
+        sum_y = (f[0] - f[1]) + roll_x(f[0] + f[1], 1)
+        dif_y = (f[2] - f[3]) + roll_x(f[2] + f[3], 1)
+        out.append(loads.load(c, z=z) - ((sum_y - dif_y) + roll_y(sum_y + dif_y, 1)))
     return out
 
 
@@ -302,27 +312,23 @@
 LOWER, UPPER = (0, 1), (6, 7)
 
 
-def solve_side(lower, z_part, given, mine, smooth, smooth_from):
+def solve_side(lower, z_part, given, mine, smoothed):
     state = [Planes(ref, 3, old) for ref, old in zip(mine, given)]
     if lower:
         fill(state, range(-3, 0), z_part=z_part)
         invert(state, -2, 0)
-        for first, last in ((-3, 0), (-2, 1), (-1, 2)):
-            spread(state, range(first, last))
-            stress(state, first, last, join=True)
-            if last < 2:
-                relax(state, range(first + 1, last + 1))
+        rounds = ((-3, 0), (-2, 1), (-1, 2))
     else:
         fill(state, range(8, 12), z_part=z_part)
         invert(state, 8, 10)
-        for first, last in ((7, 11), (6, 10), (5, 9)):
-            spread(state, range(first + 1, last + 1))
-            stress(state, first, last, resume=True)
-            if last > 9:
-                relax(state, range(first, last))
-    for k, z in enumerate(LOWER if lower else UPPER):
-        for c in range(3):
-            smooth[c, smooth_from + k] = state[0].load(c, z=z)[:ROWS]
+        rounds = ((7, 11), (6, 10), (5, 9))
+    for step, (first, last) in enumerate(rounds):
+        spread(state, range(first, last) if lower else range(first + 1, last + 1))
+        stress(state, first, last, join=lower, resume=not lower)
+        if step < 2:
+            relax(state, range(first + 1, last + 1) if lower else range(first, last))
+        if step == 1:
+            smoothed()
     return {z: misfit(state, z) for z in ((0, 1, 2) if lower else (5, 6, 7, 8))}
 
 
@@ -434,7 +440,12 @@
 
         @pl.when(is_even("slab") != lower)
         def side(given=given, middle=middle):
-            residual = solve_side(lower, z_first, given, mine, smooth, 0)
+            def smoothed():
+                for k, z in enumerate(LOWER if lower else UPPER):
+                    for c in range(3):
+                        smooth[c, k] = mine[0][c, z + 3, :ROWS, :]
+
+            residual = solve_side(lower, z_first, given, mine, smoothed)
             coarse_rows = restrict(
                 0 if lower else 1, with_middle(residual, middle), labels, chosen,
                 y_above[DOWN_SIZE : DOWN_SIZE + 1, :], z_label(z_first), rows,
@@ -445,7 +456,7 @@
 
 def solve_far(labels, chosen, y_above, z_second, *refs):
     states, (near_smooth, near_coarse) = (refs[:7], refs[7:14]), refs[14:16]
-    (smooth, coarse), rows, mine = refs[16:18], refs[18], refs[19:25]
+    (smooth, coarse), rows, mine, sems = refs[16:18], refs[18], refs[19:25], refs[25]
 
     for lower in (True, False):
         *given, middle = states[lower]
@@ -453,12 +464,18 @@
         @pl.when(is_even("slab") == lower)
         def side(given=given, middle=middle):
             near, far, kz = (UPPER, LOWER, 0) if lower else (LOWER, UPPER, 1)
-            for c in range(3):
-                for z in range(2, 6):
-                    smooth[c, z] = given[0][c, z, :ROWS, :]
-                for k, z in enumerate(near):
-                    smooth[c, z] = near_smooth[c, k]
-            residual = solve_side(lower, z_second, given, mine, smooth, far[0])
+            planes = slice(far[0] + 3, far[1] + 4)
+            copies = [
+                pltpu.make_async_copy(src, smooth.at[:, out], sems.at[k])
+                for k, (src, out) in enumerate((
+                    (given[0].at[:, 2:6, :ROWS, :], slice(2, 6)),
+                    (near_smooth, slice(near[0], near[1] + 1)),
+                    (mine[0].at[:, planes, :ROWS, :], slice(far[0], far[1] + 1)),
+                ))
+            ]
+            copies[0].start()
+            copies[1].start()
+            residual = solve_side(lower, z_second, given, mine, copies[2].start)
             coarse_rows = restrict(
                 kz, with_middle(residual, middle), labels, chosen,
                 y_above[DOWN_SIZE : DOWN_SIZE + 1, :], z_label(z_second), rows,
@@ -466,6 +483,8 @@
             for k in range(6):
                 coarse[k, kz : kz + 1, :] = coarse_rows[k]
                 coarse[k, 1 - kz : 2 - kz, :] = near_coarse[k : k + 1, :]
+            for copy in copies:
+                copy.wait()
 
 
 VMEM = pl.BlockSpec(memory_space=pltpu.VMEM)
@@ -490,24 +509,31 @@
     hbm = pl.BlockSpec(memory_space=pltpu.MemorySpace.HBM)
     blocks = [f32(3, DEPTH, ROWS, WIDTH), f32(3, DEPTH, ROWS, WIDTH), f32(DEPTH, ROWS, WIDTH)]
     arguments = (seg_y, seg_z, seg_x, field_init, load, modulus)
-    up, down, field_init, load, modulus, labels = pl.pallas_call(
+    first, second, field_init, load, modulus, labels = pl.pallas_call(
         pack_y,
-        out_shape=[f32(UP_SIZE, WIDTH), f32(DOWN_SIZE + 8, WIDTH)] + blocks + [f32(8, WIDTH)],
+        out_shape=[f32(DOWN_SIZE + 8, WIDTH), f32(DOWN_SIZE + 8, WIDTH)] + blocks + [f32(8, WIDTH)],
         in_specs=[hbm] * 6,
         out_specs=[VMEM] * 6,
         scratch_shapes=[
+            scratch(DOWN_SIZE + 8, WIDTH),
+            scratch(DOWN_SIZE + 8, WIDTH),
             pltpu.SMEM((ROWS,), jnp.int32),
             pltpu.SMEM((DEPTH,), jnp.int32),
             pltpu.VMEM((WIDTH,), jnp.int32),
-            pltpu.SemaphoreType.DMA((6,)),
+            pltpu.SemaphoreType.DMA((10,)),
         ],
         compiler_params=limit(4),
         name="pack_y",
     )(*[pltpu.with_memory_space_constraint(value, pltpu.MemorySpace.HBM) for value in arguments])
-    steps = [(i, i + 1) for i in range(lax.axis_size("sub") - 1)]
-    y_above = lax.ppermute(down, "sub", [(j, i) for i, j in steps])
-    y_below = lax.ppermute(up, "sub", steps)
-    y_parts = (y_below, y_above)
+    slabs, subs = lax.axis_size("slab"), lax.axis_size("sub")
+    down = [(s * subs + i + 1, s * subs + i) for s in range(1, slabs) for i in range(subs - 1)]
+    up = [(j, i) for i, j in down]
+    swaps = [[(i, i + 1) for i in range(start, subs - 1, 2)] for start in (0, 1)]
+    swaps = [pairs + [(j, i) for i, j in pairs] for pairs in swaps]
+    both = ("slab", "sub")
+    y_parts = (
+        lax.ppermute(first, both, down + swaps[0]), lax.ppermute(second, both, up + swaps[1])
+    )
     chosen = pl.pallas_call(
         prepare,
         out_shape=jax.ShapeDtypeStruct((WIDTH, WIDTH), jnp.bfloat16),
@@ -516,11 +542,11 @@
         compiler_params=limit(1),
         name="prepare",
     )(labels)
-    first, second = pl.pallas_call(
+    first, second, y_below, y_above = pl.pallas_call(
         pack_z,
-        out_shape=(f32(len(DOWN_PLANES), TALL, WIDTH),) * 2,
+        out_shape=(f32(len(DOWN_PLANES), TALL, WIDTH),) * 2 + (f32(DOWN_SIZE + 8, WIDTH),) * 2,
         in_specs=[VMEM] * 6,
-        out_specs=(VMEM, VMEM),
+        out_specs=(VMEM,) * 4,
         compiler_params=limit(4),
         name="pack_z",
     )(labels, field_init, load, modulus, *y_parts)
@@ -540,7 +566,7 @@
             in_specs=[VMEM] * 5,
             out_specs=[VMEM] * 7,
             compiler_params=limit(6),
-        )(field_init, load, modulus, *y_parts)
+        )(field_init, load, modulus, y_below, y_above)
     near = pl.pallas_call(
         solve_near,
         out_shape=(f32(3, 2, ROWS, WIDTH), f32(8, WIDTH)),
@@ -554,8 +580,9 @@
         solve_far,
         out_shape=(f32(3, DEPTH, ROWS, WIDTH), f32(6, SZ, SY * SX)),
         in_specs=[VMEM] * 20,
-        out_specs=(VMEM, VMEM),
-        scratch_shapes=[scratch(8 * SY, WIDTH)] + [scratch(*size) for size in sizes(15)],
+        out_specs=(hbm, VMEM),
+        scratch_shapes=[scratch(8 * SY, WIDTH)] + [scratch(*size) for size in sizes(15)]
+        + [pltpu.SemaphoreType.DMA((3,))],
         compiler_params=limit(14),
         name="solve_far",
     )(labels, chosen, y_above, z_second, *states, *near)

time: 32.5 us -> 32 us (0.985)
  the two profiles are of different devices: /device:TPU:1 before, /device:TPU:65 now
where the time goes in v2:
time: 32 us; the launch traced here: 31.8 us
  starting transfers between devices  19.9 us (62%)
  Pallas kernels  6.36 us (20%)
  waiting for transfers between devices  4.74 us (15%)
  between operations  0.71 us (2%)
    ppermute x2, starting transfers between devices, swap(): return lax.ppermute(block, axis, pairs + [(j, i) for i, j in pairs])  14 us
    ppermute x1, starting transfers between devices, on_device(): lax.ppermute(second, both, up + swaps[1])  4 us
    ppermute x2, waiting for transfers between devices, swap(): return lax.ppermute(block, axis, pairs + [(j, i) for i, j in pairs])  3.08 us
    pallas_call x1, Pallas kernels, on_device(): pl.pallas_call(solve_far, out_shape=(f32(3, DEPTH, ROWS, WIDTH), f32(6, S...  2.11 us
    ppermute x1, starting transfers between devices, on_device(): lax.ppermute(first, both, down + swaps[0])  1.92 us
    pallas_call x2, Pallas kernels, on_device(): pl.pallas_call(functools.partial(solve_inner, even), out_shape=[f32(*size...  1.68 us
    ppermute x1, waiting for transfers between devices, on_device(): lax.ppermute(second, both, up + swaps[1])  1.55 us
    pallas_call x1, Pallas kernels, on_device(): pl.pallas_call(solve_near, out_shape=(f32(3, 2, ROWS, WIDTH), f32(8, WIDT...  1.3 us
  transfers between devices with their start and end apart: 4, of which 3 were waited for; matrix products, arithmetic and copies ran while one was open for 0% of the time, Pallas kernels for 9%

profile of v2, /device:TPU:65, one launch (start us, length us, event | category | flops | bytes accessed | tf_op | source)
XLA Modules:
  0.0 31.8 jit_solution(9517539870806966914)
XLA Ops:
  0.6 1.2 %pack_y.1 = (f32[200,128]{1,0:T(8,128)S(1)}, f32[200,128]{1,0:T(8,128)S(1)}, f32[3,8,16,128]{3,2,1,0:T(8,128)S(1)}, f32[3,8,16,128]{3,2,1,0:T(8,128)S(1)}, f32[8...) custom-call(s32[16]{0:T(128)} %seg_y_hbm.1, s32[8]{0:T(128)} %seg_z_hbm.1, s32[128]{0:T(128)} %seg_x_hbm.1, ...), custom_call_target="tpu_custom_call" | custom-call | tf_op jit(solution)/shard_map/pack_y/pallas_call | solution.py:512
  1.8 1.9 %collective-permute-start = (f32[200,128]{1,0:T(8,128)S(1)}, f32[200,128]{1,0:T(8,128)S(1)}, u32[]{:S(2)}, u32[]{:S(2)}) collective-permute-start(f32[200,128]{1,0:T(8,128)S(1)} %get-tuple-element.32), channel_id=1, source_target_pairs={{13,12},{14,13},{15,14},{16,15},{17,16},{18,17},{19,18},{20,19},{2... | collective-permute-start | bytes 307208 | tf_op jit(solution)/shard_map/ppermute | solution.py:535
  3.7 4.0 %collective-permute-start.1 = (f32[200,128]{1,0:T(8,128)S(1)}, f32[200,128]{1,0:T(8,128)S(1)}, u32[]{:S(2)}, u32[]{:S(2)}) collective-permute-start(f32[200,128]{1,0:T(8,128)S(1)} %get-tuple-element.33), channel_id=1, source_target_pairs={{12,13},{13,14},{14,15},{15,16},{16,17},{17,18},{18,19},{19,20},{2... | collective-permute-start | bytes 307208 | tf_op jit(solution)/shard_map/ppermute | solution.py:535
  7.8 0.1 collective-permute-done.y_first
  7.9 1.5 %collective-permute-done.1.y_second = f32[200,128]{1,0:T(8,128)S(1)} collective-permute-done((f32[200,128]{1,0:T(8,128)S(1)}, f32[200,128]{1,0:T(8,128)S(1)}, u32[]{:S(2)}, u32[]{:S(2)}) %collective-permute-start.1) | collective-permute-done | bytes 102432 | tf_op jit(solution)/shard_map/ppermute | solution.py:535
  9.4 0.1 pack_z.1
  9.5 12.1 %collective-permute-start.3 = (f32[24,24,128]{2,1,0:T(8,128)S(1)}, f32[24,24,128]{2,1,0:T(8,128)S(1)}, u32[]{:S(2)}, u32[]{:S(2)}) collective-permute-start(f32[24,24,128]{2,1,0:T(8,128)S(1)} %get-tuple-element.51), channel_id=1, source_target_pairs={{0,12},{24,36},{48,60},{72,84},{96,108},{120,132},{144,156},{168,1... | collective-permute-start | bytes 884744 | tf_op jit(solution)/shard_map/ppermute | solution.py:504
  21.6 1.9 %collective-permute-start.2 = (f32[24,24,128]{2,1,0:T(8,128)S(1)}, f32[24,24,128]{2,1,0:T(8,128)S(1)}, u32[]{:S(2)}, u32[]{:S(2)}) collective-permute-start(f32[24,24,128]{2,1,0:T(8,128)S(1)} %get-tuple-element.35), channel_id=1, source_target_pairs={{12,24},{36,48},{60,72},{84,96},{108,120},{132,144},{156,168},{180... | collective-permute-start | bytes 884744 | tf_op jit(solution)/shard_map/ppermute | solution.py:504
  23.6 1.7 %shard_map.77 = (f32[3,8,24,128]{3,2,1,0:T(8,128)S(1)}, f32[3,8,24,128]{3,2,1,0:T(8,128)S(1)}, f32[8,24,128]{2,1,0:T(8,128)S(1)}, f32[6,8,24,128]{3,2,1,0:T(8,12...) custom-call(f32[3,8,16,128]{3,2,1,0:T(8,128)S(1)} %get-tuple-element.29.field., ...), custom_call_target="tpu_custom_call" | custom-call | tf_op jit(solution)/shard_map/pallas_call | solution.py:563
  25.2 0.0 collective-permute-done.3.z_first
  25.3 1.3 %solve_near.1 = (f32[3,2,16,128]{3,2,1,0:T(8,128)S(1)}, f32[8,128]{1,0:T(8,128)S(1)}) custom-call(f32[8,128]{1,0:T(8,128)S(1)} %get-tuple-element.28.labels, bf16[128,128]{1,0:T(8,128)(2,1)S(1)} %prepare.1.chosen, f32[200,128]{1,0:T(8,128)S(1)} %get-tuple-element.34.refs_4_.y_above, f32[24,24,128]{2,1,0:T(8,128)S(1)} %collective-permute-done.3.z_first, ...), custom_call_target="tpu_custom_call" | custom-call | tf_op jit(solution)/shard_map/solve_near/pallas_call | solution.py:570
  26.6 3.1 %collective-permute-done.2.z_second = f32[24,24,128]{2,1,0:T(8,128)S(1)} collective-permute-done((f32[24,24,128]{2,1,0:T(8,128)S(1)}, f32[24,24,128]{2,1,0:T(8,128)S(1)}, u32[]{:S(2)}, u32[]{:S(2)}) %collective-permute-start.2) | collective-permute-done | bytes 294944 | tf_op jit(solution)/shard_map/ppermute | solution.py:504
  29.6 2.1 %solve_far.1 = (f32[3,8,16,128]{3,2,1,0:T(8,128)}, f32[6,2,128]{2,1,0:T(2,128)}) custom-call(f32[8,128]{1,0:T(8,128)S(1)} %get-tuple-element.28.labels, bf16[128,128]{1,0:T(8,128)(2,1)S(1)} %prepare.1.chosen, f32[200,128]{1,0:T(8,128)S(1)} %get-tuple-element.34.refs_4_.y_above, f32[24,24,128]{2,1,0:T(8,128)S(1)} %collective-permute-done.2.z_second, ...), custom_call_target="tpu_custom_call" | custom-call | tf_op jit(solution)/shard_map/solve_far/pallas_call | solution.py:579
  (2 shorter events, 0.0 us)
Async XLA Ops:
  1.8 6.0 %collective-permute-start = (f32[200,128]{1,0:T(8,128)S(1)}, f32[200,128]{1,0:T(8,128)S(1)}, u32[]{:S(2)}, u32[]{:S(2)}) collective-permute-start(f32[200,128]{1,0:T(8,128)S(1)} %get-tuple-element.32), channel_id=1, source_target_pairs={{13,12},{14,13},{15,14},{16,15},{17,16},{18,17},{19,18},{20,19},{2... | collective-permute-start | bytes 307208 | tf_op jit(solution)/shard_map/ppermute | solution.py:535
  3.7 5.7 %collective-permute-start.1 = (f32[200,128]{1,0:T(8,128)S(1)}, f32[200,128]{1,0:T(8,128)S(1)}, u32[]{:S(2)}, u32[]{:S(2)}) collective-permute-start(f32[200,128]{1,0:T(8,128)S(1)} %get-tuple-element.33), channel_id=1, source_target_pairs={{12,13},{13,14},{14,15},{15,16},{16,17},{17,18},{18,19},{19,20},{2... | collective-permute-start | bytes 307208 | tf_op jit(solution)/shard_map/ppermute | solution.py:535
  9.5 15.8 %collective-permute-start.3 = (f32[24,24,128]{2,1,0:T(8,128)S(1)}, f32[24,24,128]{2,1,0:T(8,128)S(1)}, u32[]{:S(2)}, u32[]{:S(2)}) collective-permute-start(f32[24,24,128]{2,1,0:T(8,128)S(1)} %get-tuple-element.51), channel_id=1, source_target_pairs={{0,12},{24,36},{48,60},{72,84},{96,108},{120,132},{144,156},{168,1... | collective-permute-start | bytes 884744 | tf_op jit(solution)/shard_map/ppermute | solution.py:504
  21.6 8.0 %collective-permute-start.2 = (f32[24,24,128]{2,1,0:T(8,128)S(1)}, f32[24,24,128]{2,1,0:T(8,128)S(1)}, u32[]{:S(2)}, u32[]{:S(2)}) collective-permute-start(f32[24,24,128]{2,1,0:T(8,128)S(1)} %get-tuple-element.35), channel_id=1, source_target_pairs={{12,24},{36,48},{60,72},{84,96},{108,120},{132,144},{156,168},{180... | collective-permute-start | bytes 884744 | tf_op jit(solution)/shard_map/ppermute | solution.py:504

commit v3 on v2

--- a/solution.py
+++ b/solution.py
@@ -54,24 +54,25 @@
     seg_y_hbm, seg_z_hbm, seg_x_hbm, field_hbm, load_hbm, modulus_hbm,
     first, second, field, load, modulus, labels, up, down, seg_y, seg_z, seg_x, sems,
 ):
-    pairs = [(field_hbm.at[c], field.at[c]) for c in range(3)]
-    pairs += [(load_hbm.at[c], load.at[c]) for c in range(3)]
-    pairs += [
-        (modulus_hbm, modulus), (seg_y_hbm, seg_y), (seg_z_hbm, seg_z), (seg_x_hbm, seg_x),
-    ]
+    pairs = (
+        (field_hbm, field), (load_hbm, load), (modulus_hbm, modulus),
+        (seg_y_hbm, seg_y), (seg_z_hbm, seg_z), (seg_x_hbm, seg_x),
+    )
     copies = [pltpu.make_async_copy(src, dst, sems.at[k]) for k, (src, dst) in enumerate(pairs)]
     for copy in copies:
         copy.start()
     for ref, kind in ((field, FIELD), (load, LOAD), (modulus, MODULUS)):
+        copies[kind].wait()
         for c in range(1 if kind == MODULUS else 3):
-            copies[3 * kind + c].wait()
             for z in range(DEPTH):
                 at = (z,) if kind == MODULUS else (c, z)
                 up[y_rows(kind, c, z, True), :] = ref[(*at, slice(ROWS - UP_ROWS[kind], ROWS), slice(None))]
                 down[y_rows(kind, c, z, False), :] = ref[(*at, slice(0, DOWN_ROWS[kind]), slice(None))]
-    for copy in copies[7:]:
+    for copy in copies[3:]:
         copy.wait()
-    down[DOWN_SIZE:, :] = jnp.full((8, WIDTH), seg_y[0].astype(jnp.float32))
+    lane = lax.broadcasted_iota(jnp.int32, (DOWN_ROWS[MODULUS], WIDTH), 1)
+    at = y_rows(*LABEL_PLANE, False)
+    down[at, :] = jnp.where(lane == WIDTH - 1, seg_y[0].astype(jnp.float32), down[at, :])
     upward = (lax.axis_index("slab") == 0) & is_even("sub")
     first[...] = jnp.where(upward, up[...], down[...])
     second[...] = jnp.where(upward, down[...], up[...])
@@ -215,7 +216,7 @@
             modes.store(dif_left - dif_y, 4 * c + 3, z=z)
 
 
-def stress(state, lo, hi, resume=False, join=False):
+def stress(state, lo, hi, resume=False, join=False, low_end=True, high_end=True):
     elem, modes, forces = state[2], state[4], state[5]
     for tile in range(3):
         old = [modes.load(k, z=lo, tile=tile) for k in range(12)]
@@ -249,15 +250,16 @@
                 yz, mu1 * (q + ye), s_z + mu0 * yf, last_scale * yg,
                 t + twice * zd, s_x + mu0 * ze, s_y + mu0 * zf, last_scale * zg,
             )
-            for k in range(12):
+            for k in range(12 if z > lo or low_end else 0):
                 if even[k] is None:
                     low = -odd[k] if held is None else held[k] - odd[k]
                 else:
                     low = even[k] - odd[k] if held is None else held[k] + (even[k] - odd[k])
                 forces.store(low, k, z=z, tile=tile)
-            held = [odd[k] if even[k] is None else even[k] + odd[k] for k in range(12)]
+            if z < hi - 1 or high_end:
+                held = [odd[k] if even[k] is None else even[k] + odd[k] for k in range(12)]
             old = new
-        for k in range(12):
+        for k in range(12 if high_end else 0):
             total = forces.load(k, z=hi, tile=tile) + held[k] if join else held[k]
             forces.store(total, k, z=hi, tile=tile)
 
@@ -324,7 +326,7 @@
         rounds = ((7, 11), (6, 10), (5, 9))
     for step, (first, last) in enumerate(rounds):
         spread(state, range(first, last) if lower else range(first + 1, last + 1))
-        stress(state, first, last, join=lower, resume=not lower)
+        stress(state, first, last, join=lower, resume=not lower, low_end=not lower, high_end=lower)
         if step < 2:
             relax(state, range(first + 1, last + 1) if lower else range(first, last))
         if step == 1:
@@ -423,9 +425,12 @@
     return [value * scale for value in s[:3] + turned]
 
 
+def last_lane(row):
+    return jnp.broadcast_to(row[:, WIDTH - 1 :], (1, WIDTH))
+
+
 def z_label(part):
-    row = part[DOWN_PLANES.index(LABEL_PLANE), 0:1, :]
-    return jnp.broadcast_to(row[:, WIDTH - 1 :], (1, WIDTH))
+    return last_lane(part[DOWN_PLANES.index(LABEL_PLANE), 0:1, :])
 
 
 def with_middle(residual, middle):
@@ -448,7 +453,7 @@
             residual = solve_side(lower, z_first, given, mine, smoothed)
             coarse_rows = restrict(
                 0 if lower else 1, with_middle(residual, middle), labels, chosen,
-                y_above[DOWN_SIZE : DOWN_SIZE + 1, :], z_label(z_first), rows,
+                last_lane(y_above[DOWN_AT[MODULUS] : DOWN_AT[MODULUS] + 1, :]), z_label(z_first), rows,
             )
             for k in range(6):
                 coarse[k : k + 1, :] = coarse_rows[k]
@@ -478,7 +483,7 @@
             residual = solve_side(lower, z_second, given, mine, copies[2].start)
             coarse_rows = restrict(
                 kz, with_middle(residual, middle), labels, chosen,
-                y_above[DOWN_SIZE : DOWN_SIZE + 1, :], z_label(z_second), rows,
+                last_lane(y_above[DOWN_AT[MODULUS] : DOWN_AT[MODULUS] + 1, :]), z_label(z_second), rows,
             )
             for k in range(6):
                 coarse[k, kz : kz + 1, :] = coarse_rows[k]
@@ -511,16 +516,16 @@
     arguments = (seg_y, seg_z, seg_x, field_init, load, modulus)
     first, second, field_init, load, modulus, labels = pl.pallas_call(
         pack_y,
-        out_shape=[f32(DOWN_SIZE + 8, WIDTH), f32(DOWN_SIZE + 8, WIDTH)] + blocks + [f32(8, WIDTH)],
+        out_shape=[f32(DOWN_SIZE, WIDTH), f32(DOWN_SIZE, WIDTH)] + blocks + [f32(8, WIDTH)],
         in_specs=[hbm] * 6,
         out_specs=[VMEM] * 6,
         scratch_shapes=[
-            scratch(DOWN_SIZE + 8, WIDTH),
-            scratch(DOWN_SIZE + 8, WIDTH),
+            scratch(DOWN_SIZE, WIDTH),
+            scratch(DOWN_SIZE, WIDTH),
             pltpu.SMEM((ROWS,), jnp.int32),
             pltpu.SMEM((DEPTH,), jnp.int32),
             pltpu.VMEM((WIDTH,), jnp.int32),
-            pltpu.SemaphoreType.DMA((10,)),
+            pltpu.SemaphoreType.DMA((6,)),
         ],
         compiler_params=limit(4),
         name="pack_y",
@@ -544,7 +549,7 @@
     )(labels)
     first, second, y_below, y_above = pl.pallas_call(
         pack_z,
-        out_shape=(f32(len(DOWN_PLANES), TALL, WIDTH),) * 2 + (f32(DOWN_SIZE + 8, WIDTH),) * 2,
+        out_shape=(f32(len(DOWN_PLANES), TALL, WIDTH),) * 2 + (f32(DOWN_SIZE, WIDTH),) * 2,
         in_specs=[VMEM] * 6,
         out_specs=(VMEM,) * 4,
         compiler_params=limit(4),

time: 32 us -> 31.9 us (level)
  transfers between devices with their start and end apart: 4 -> 4, of which waited for: 3 -> 3; matrix products, arithmetic and copies ran while one was open for 0% -> 0% of each run, Pallas kernels for 9% -> 10%
where the time goes in v3:
time: 31.9 us; the launch traced here: 31.7 us
  starting transfers between devices  19.9 us (62%)
  Pallas kernels  6.39 us (20%)
  waiting for transfers between devices  4.67 us (15%)
  between operations  0.71 us (2%)
    ppermute x2, starting transfers between devices, swap(): return lax.ppermute(block, axis, pairs + [(j, i) for i, j in pairs])  14 us
    ppermute x1, starting transfers between devices, on_device(): lax.ppermute(second, both, up + swaps[1])  4 us
    ppermute x2, waiting for transfers between devices, swap(): return lax.ppermute(block, axis, pairs + [(j, i) for i, j in pairs])  3.05 us
    pallas_call x1, Pallas kernels, on_device(): pl.pallas_call(solve_far, out_shape=(f32(3, DEPTH, ROWS, WIDTH), f32(6, S...  2.14 us
    ppermute x1, starting transfers between devices, on_device(): lax.ppermute(first, both, down + swaps[0])  1.92 us
    pallas_call x2, Pallas kernels, on_device(): pl.pallas_call(functools.partial(solve_inner, even), out_shape=[f32(*size...  1.7 us
    ppermute x1, waiting for transfers between devices, on_device(): lax.ppermute(second, both, up + swaps[1])  1.55 us
    pallas_call x1, Pallas kernels, on_device(): pl.pallas_call(solve_near, out_shape=(f32(3, 2, ROWS, WIDTH), f32(8, WIDT...  1.31 us
  transfers between devices with their start and end apart: 4, of which 3 were waited for; matrix products, arithmetic and copies ran while one was open for 0% of the time, Pallas kernels for 10%

profile of v3, /device:TPU:65, one launch (start us, length us, event | category | flops | bytes accessed | tf_op | source)
XLA Modules:
  0.0 31.7 jit_solution(17368056020283694813)
XLA Ops:
  0.6 1.2 %pack_y.1 = (f32[192,128]{1,0:T(8,128)S(1)}, f32[192,128]{1,0:T(8,128)S(1)}, f32[3,8,16,128]{3,2,1,0:T(8,128)S(1)}, f32[3,8,16,128]{3,2,1,0:T(8,128)S(1)}, f32[8...) custom-call(s32[16]{0:T(128)} %seg_y_hbm.1, s32[8]{0:T(128)} %seg_z_hbm.1, s32[128]{0:T(128)} %seg_x_hbm.1, ...), custom_call_target="tpu_custom_call" | custom-call | tf_op jit(solution)/shard_map/pack_y/pallas_call | solution.py:517
  1.8 1.9 %collective-permute-start = (f32[192,128]{1,0:T(8,128)S(1)}, f32[192,128]{1,0:T(8,128)S(1)}, u32[]{:S(2)}, u32[]{:S(2)}) collective-permute-start(f32[192,128]{1,0:T(8,128)S(1)} %get-tuple-element.32), channel_id=1, source_target_pairs={{13,12},{14,13},{15,14},{16,15},{17,16},{18,17},{19,18},{20,19},{2... | collective-permute-start | bytes 294920 | tf_op jit(solution)/shard_map/ppermute | solution.py:540
  3.7 4.0 %collective-permute-start.1 = (f32[192,128]{1,0:T(8,128)S(1)}, f32[192,128]{1,0:T(8,128)S(1)}, u32[]{:S(2)}, u32[]{:S(2)}) collective-permute-start(f32[192,128]{1,0:T(8,128)S(1)} %get-tuple-element.33), channel_id=1, source_target_pairs={{12,13},{13,14},{14,15},{15,16},{16,17},{17,18},{18,19},{19,20},{2... | collective-permute-start | bytes 294920 | tf_op jit(solution)/shard_map/ppermute | solution.py:540
  7.7 0.1 collective-permute-done.y_first
  7.8 1.6 %collective-permute-done.1.y_second = f32[192,128]{1,0:T(8,128)S(1)} collective-permute-done((f32[192,128]{1,0:T(8,128)S(1)}, f32[192,128]{1,0:T(8,128)S(1)}, u32[]{:S(2)}, u32[]{:S(2)}) %collective-permute-start.1) | collective-permute-done | bytes 98336 | tf_op jit(solution)/shard_map/ppermute | solution.py:540
  9.3 0.1 pack_z.1
  9.4 12.1 %collective-permute-start.3 = (f32[24,24,128]{2,1,0:T(8,128)S(1)}, f32[24,24,128]{2,1,0:T(8,128)S(1)}, u32[]{:S(2)}, u32[]{:S(2)}) collective-permute-start(f32[24,24,128]{2,1,0:T(8,128)S(1)} %get-tuple-element.51), channel_id=1, source_target_pairs={{0,12},{24,36},{48,60},{72,84},{96,108},{120,132},{144,156},{168,1... | collective-permute-start | bytes 884744 | tf_op jit(solution)/shard_map/ppermute | solution.py:509
  21.5 1.9 %collective-permute-start.2 = (f32[24,24,128]{2,1,0:T(8,128)S(1)}, f32[24,24,128]{2,1,0:T(8,128)S(1)}, u32[]{:S(2)}, u32[]{:S(2)}) collective-permute-start(f32[24,24,128]{2,1,0:T(8,128)S(1)} %get-tuple-element.35), channel_id=1, source_target_pairs={{12,24},{36,48},{60,72},{84,96},{108,120},{132,144},{156,168},{180... | collective-permute-start | bytes 884744 | tf_op jit(solution)/shard_map/ppermute | solution.py:509
  23.5 1.7 %shard_map.77 = (f32[3,8,24,128]{3,2,1,0:T(8,128)S(1)}, f32[3,8,24,128]{3,2,1,0:T(8,128)S(1)}, f32[8,24,128]{2,1,0:T(8,128)S(1)}, f32[6,8,24,128]{3,2,1,0:T(8,12...) custom-call(f32[3,8,16,128]{3,2,1,0:T(8,128)S(1)} %get-tuple-element.29.field., ...), custom_call_target="tpu_custom_call" | custom-call | tf_op jit(solution)/shard_map/pallas_call | solution.py:568
  25.2 0.0 collective-permute-done.3.z_first
  25.2 1.3 %solve_near.1 = (f32[3,2,16,128]{3,2,1,0:T(8,128)S(1)}, f32[8,128]{1,0:T(8,128)S(1)}) custom-call(f32[8,128]{1,0:T(8,128)S(1)} %get-tuple-element.28.labels, bf16[128,128]{1,0:T(8,128)(2,1)S(1)} %prepare.1.chosen, f32[192,128]{1,0:T(8,128)S(1)} %get-tuple-element.34.refs_4_.y_above, f32[24,24,128]{2,1,0:T(8,128)S(1)} %collective-permute-done.3.z_first, ...), custom_call_target="tpu_custom_call" | custom-call | tf_op jit(solution)/shard_map/solve_near/pallas_call | solution.py:575
  26.5 3.0 %collective-permute-done.2.z_second = f32[24,24,128]{2,1,0:T(8,128)S(1)} collective-permute-done((f32[24,24,128]{2,1,0:T(8,128)S(1)}, f32[24,24,128]{2,1,0:T(8,128)S(1)}, u32[]{:S(2)}, u32[]{:S(2)}) %collective-permute-start.2) | collective-permute-done | bytes 294944 | tf_op jit(solution)/shard_map/ppermute | solution.py:509
  29.6 2.1 %solve_far.1 = (f32[3,8,16,128]{3,2,1,0:T(8,128)}, f32[6,2,128]{2,1,0:T(2,128)}) custom-call(f32[8,128]{1,0:T(8,128)S(1)} %get-tuple-element.28.labels, bf16[128,128]{1,0:T(8,128)(2,1)S(1)} %prepare.1.chosen, f32[192,128]{1,0:T(8,128)S(1)} %get-tuple-element.34.refs_4_.y_above, f32[24,24,128]{2,1,0:T(8,128)S(1)} %collective-permute-done.2.z_second, ...), custom_call_target="tpu_custom_call" | custom-call | tf_op jit(solution)/shard_map/solve_far/pallas_call | solution.py:584
  (2 shorter events, 0.0 us)
Async XLA Ops:
  1.8 6.0 %collective-permute-start = (f32[192,128]{1,0:T(8,128)S(1)}, f32[192,128]{1,0:T(8,128)S(1)}, u32[]{:S(2)}, u32[]{:S(2)}) collective-permute-start(f32[192,128]{1,0:T(8,128)S(1)} %get-tuple-element.32), channel_id=1, source_target_pairs={{13,12},{14,13},{15,14},{16,15},{17,16},{18,17},{19,18},{20,19},{2... | collective-permute-start | bytes 294920 | tf_op jit(solution)/shard_map/ppermute | solution.py:540
  3.7 5.6 %collective-permute-start.1 = (f32[192,128]{1,0:T(8,128)S(1)}, f32[192,128]{1,0:T(8,128)S(1)}, u32[]{:S(2)}, u32[]{:S(2)}) collective-permute-start(f32[192,128]{1,0:T(8,128)S(1)} %get-tuple-element.33), channel_id=1, source_target_pairs={{12,13},{13,14},{14,15},{15,16},{16,17},{17,18},{18,19},{19,20},{2... | collective-permute-start | bytes 294920 | tf_op jit(solution)/shard_map/ppermute | solution.py:540
  9.4 15.8 %collective-permute-start.3 = (f32[24,24,128]{2,1,0:T(8,128)S(1)}, f32[24,24,128]{2,1,0:T(8,128)S(1)}, u32[]{:S(2)}, u32[]{:S(2)}) collective-permute-start(f32[24,24,128]{2,1,0:T(8,128)S(1)} %get-tuple-element.51), channel_id=1, source_target_pairs={{0,12},{24,36},{48,60},{72,84},{96,108},{120,132},{144,156},{168,1... | collective-permute-start | bytes 884744 | tf_op jit(solution)/shard_map/ppermute | solution.py:509
  21.5 8.0 %collective-permute-start.2 = (f32[24,24,128]{2,1,0:T(8,128)S(1)}, f32[24,24,128]{2,1,0:T(8,128)S(1)}, u32[]{:S(2)}, u32[]{:S(2)}) collective-permute-start(f32[24,24,128]{2,1,0:T(8,128)S(1)} %get-tuple-element.35), channel_id=1, source_target_pairs={{12,24},{36,48},{60,72},{84,96},{108,120},{132,144},{156,168},{180... | collective-permute-start | bytes 884744 | tf_op jit(solution)/shard_map/ppermute | solution.py:509
